TPU v7x, 32 devices: a whole 2x2x4 slice. The times are simulated.
32 devices in a mesh: ctx: 8 (over z, x), fsdp: 4 (over y, core).
Axes of the slice: x: 2, y: 2, z: 4, core: 2. Of those that a mesh axis runs over, the one named last changes fastest.
Arguments:
- inputs: bfloat16 [4, 4096, 768], P('fsdp', 'ctx'), may hold values from -6 to 6
- doc_starts: int32 [4, 8], P('fsdp'), may hold values from 0 to 4095, as said below
- qkv_weight: bfloat16 [768, 2304], P('fsdp'), may hold values from -0.21875 to 0.21875
- query_bias: bfloat16 [768], P('fsdp'), may hold values from -3 to 3
- value_bias: bfloat16 [768], P('fsdp'), may hold values from -3 to 3
- out_weight: bfloat16 [768, 768], P('fsdp'), may hold values from -2 to 2
- out_bias: bfloat16 [768], P('fsdp'), may hold values from -2 to 2
- norm1_gain: bfloat16 [768], P('fsdp'), may hold values from 0.25 to 1.75
- norm1_bias: bfloat16 [768], P('fsdp'), may hold values from -2 to 2
- in_weight: bfloat16 [768, 3072], P('fsdp'), may hold values from -0.21875 to 0.21875
- in_bias: bfloat16 [3072], P('fsdp'), may hold values from -3 to 3
- back_weight: bfloat16 [3072, 768], P('fsdp'), may hold values from -0.109375 to 0.109375
- back_bias: bfloat16 [768], P('fsdp'), may hold values from -2 to 2
- norm2_gain: bfloat16 [768], P('fsdp'), may hold values from 0.25 to 1.75
- norm2_bias: bfloat16 [768], P('fsdp'), may hold values from -2 to 2
- cotangent: bfloat16 [4, 4096, 768], P('fsdp', 'ctx'), may hold values from -6 to 6
Outputs:
- output: bfloat16 [4, 4096, 768], P('fsdp', 'ctx')
- input_grad: float32 [4, 4096, 768], P('fsdp', 'ctx')
- qkv_weight_grad: float32 [768, 2304], P('fsdp')
- query_bias_grad: float32 [768], P('fsdp')
- value_bias_grad: float32 [768], P('fsdp')
- out_weight_grad: float32 [768, 768], P('fsdp')
- out_bias_grad: float32 [768], P('fsdp')
- norm1_gain_grad: float32 [768], P('fsdp')
- norm1_bias_grad: float32 [768], P('fsdp')
- in_weight_grad: float32 [768, 3072], P('fsdp')
- in_bias_grad: float32 [3072], P('fsdp')
- back_weight_grad: float32 [3072, 768], P('fsdp')
- back_bias_grad: float32 [768], P('fsdp')
- norm2_gain_grad: float32 [768], P('fsdp')
- norm2_bias_grad: float32 [768], P('fsdp')
Inputs may be any that keep to these rules, and one draw needn't show every extreme that they name: `doc_starts`: row s lists the first positions of the 8 documents of stream s in increasing order, all different; the first is 0 and the last is 4095, a one-token document at the stream's end. A document runs from its start to the next start.
All inputs are finite; a program needn't handle non-finite values.
Results may differ from a plain program's by a relative error of at most 0.022.
Values may be sent and summed in bfloat16 or wider, within the bound.
No kernel may reach another device: no remote copies, remote signals or barrier semaphores. Data moves between devices by JAX's collectives and lax.ppermute only.
A program may use at most 192 MiB of HBM per device.

v0:
```python
from functools import partial
import math

import jax
import jax.numpy as jnp
from jax import lax
from jax.experimental import pallas as pl
from jax.experimental.pallas import tpu as pltpu
from jax.sharding import PartitionSpec as P

H = 12
HD = 64
EPSILON = 1e-05
BIG = 2.0**100
LOG2E = 1.4426950408889634
PAD = 16
KERNEL_FLOPS = 3_000_000_000
KERNEL_BYTES = 20_000_000


def ctx_shift(array, groups, parts, dg, ds):
    pairs = []
    for g in range(groups):
        for s in range(parts):
            pairs.append((g * parts + s, ((g + dg) % groups) * parts + (s + ds) % parts))
    return lax.ppermute(array, "ctx", pairs)


def swap(array, axis, bit):
    size = lax.axis_size(axis)
    return lax.ppermute(array, axis, [(i, i ^ (1 << bit)) for i in range(size)])


def bits_of(axis):
    return lax.axis_size(axis).bit_length() - 1


def bit_at(axis, bit):
    return (lax.axis_index(axis) >> bit) & 1


def pick(array, which, dim):
    return lax.dynamic_index_in_dim(array, which, dim, keepdims=False)


def together(*values):
    return lax.optimization_barrier(values)


def join(mine, own, other, dim):
    return jnp.where(
        mine == 0,
        jnp.concatenate([own, other], axis=dim),
        jnp.concatenate([other, own], axis=dim),
    )


def gather_top(shard):
    return swap(shard, "fsdp", bits_of("fsdp") - 1)


def gather_rest(shard, other):
    top = bits_of("fsdp") - 1
    held = join(bit_at("fsdp", top), shard[None], other[None], 0)
    for bit in reversed(range(top)):
        got = swap(held, "fsdp", bit)
        pair = join(bit_at("fsdp", bit), held[:, None], got[:, None], 1)
        held = pair.reshape((-1,) + shard.shape)
    return held


def halve(held, axis, bit, dim):
    mine = bit_at(axis, bit)
    if axis == "fsdp":
        pairs = held.reshape((held.shape[0] // 2, 2) + held.shape[1:])
        keep, send = pick(pairs, mine, 1), pick(pairs, 1 - mine, 1)
    else:
        half = held.shape[dim] // 2
        keep = lax.dynamic_slice_in_dim(held, mine * half, half, dim)
        send = lax.dynamic_slice_in_dim(held, (1 - mine) * half, half, dim)
    return add_low(keep, swap(send, axis, bit))


def add_low(a, b):
    return (a.astype(jnp.float32) + b.astype(jnp.float32)).astype(jnp.bfloat16)


def exchange(held, axis, bit):
    return add_low(held, swap(held, axis, bit))


def double(held, axis, bit, dim):
    return join(bit_at(axis, bit), held, swap(held, axis, bit), dim)


def doc_row(meta, base, length, docs):
    pos = base + lax.broadcasted_iota(jnp.int32, (1, length), 1)
    doc = jnp.full((1, length), -1, jnp.int32)
    for j in range(docs):
        doc = doc + (pos >= meta[2 + j]).astype(jnp.int32)
    return doc


def dot(a, b):
    return jnp.dot(a, b, preferred_element_type=jnp.float32)


def dot_t(a, b):
    return lax.dot_general(a, b, (((1,), (1,)), ((), ())), preferred_element_type=jnp.float32)


def fill_keys(meta, own, others, groups, parts, docs, rows, store):
    g, s = meta[0], meta[1]
    for j in range(groups):
        for e in range(parts):
            block = lax.rem(g - j + groups, groups) * parts + lax.rem(s - e + parts, parts)
            if e == 0:
                key_t, value_t = own[j][1, 0], own[j][2, 0]
            else:
                ref = others[(e - 1) * groups + j]
                key_t, value_t = ref[0, 0], ref[1, 0]
            doc = doc_row(meta, block * rows, rows, docs)
            hot = (lax.broadcasted_iota(jnp.int32, (HD, rows), 0) == doc).astype(jnp.float32)
            keys = jnp.concatenate([key_t, hot.astype(jnp.bfloat16)], axis=0)
            store(block, keys, key_t, value_t)


def query_full(meta, query_t, j, groups, parts, docs, rows):
    g, s = meta[0], meta[1]
    block = lax.rem(g - j + groups, groups) * parts + s
    doc = doc_row(meta, block * rows, rows, docs)
    shut = jnp.where(lax.broadcasted_iota(jnp.int32, (HD, rows), 0) == doc, 0.0, -BIG)
    return jnp.concatenate([query_t, shut.astype(jnp.bfloat16)], axis=0)


def attend_kernel(groups, parts, docs, rows, meta, *refs):
    own = refs[:groups]
    others = refs[groups : groups * parts]
    low_ref, wide_ref, log_ref, queries_ref, keys_ref, values_ref = refs[groups * parts :]
    coeff = LOG2E * HD**-0.5

    def store(block, keys, key_t, value_t):
        keys_ref[block] = keys.T
        values_ref[block] = value_t

    fill_keys(meta, own, others, groups, parts, docs, rows, store)
    for j in range(groups):
        queries_ref[j] = query_full(meta, own[j][0, 0], j, groups, parts, docs, rows)

    def one_slot(j, carry):
        full = queries_ref[j]

        def step(t, state):
            best, total, accum = state
            scores = dot(keys_ref[t], full)
            new_best = jnp.maximum(best, jnp.max(scores, axis=0, keepdims=True))
            weights = jnp.exp2((scores - new_best) * coeff)
            shrink = jnp.exp2((best - new_best) * coeff)
            total = total * shrink + jnp.sum(weights, axis=0, keepdims=True)
            accum = accum * shrink + dot(values_ref[t], weights.astype(jnp.bfloat16))
            return new_best, total, accum

        best, total, accum = lax.fori_loop(
            meta[2 + docs + 2 * j],
            meta[3 + docs + 2 * j],
            step,
            (
                jnp.full((1, rows), -BIG, jnp.float32),
                jnp.zeros((1, rows), jnp.float32),
                jnp.zeros((HD, rows), jnp.float32),
            ),
        )
        attended = accum / total
        at = pl.ds(pl.multiple_of(j * rows, rows), rows)
        wide_ref[0, :, at] = attended
        low_ref[0, :, at] = attended.astype(jnp.bfloat16)
        log_ref[0, :, at] = best * coeff + jnp.log2(total)
        return carry

    lax.fori_loop(0, groups, one_slot, 0)


def attend_back_kernel(groups, parts, docs, rows, meta, *refs):
    own = refs[:groups]
    others = refs[groups : groups * parts]
    grads = refs[groups * parts : groups * parts + groups]
    rest = refs[groups * parts + groups :]
    wide_ref, log_ref = rest[:2]
    dq_ref, mine_ref = rest[2:4]
    theirs = rest[4] if parts > 1 else None
    queries_ref, grads_ref, keys_ref, keys_t_ref, values_ref, accum_ref = rest[-6:]
    coeff = LOG2E * HD**-0.5

    def store(block, keys, key_t, value_t):
        keys_ref[block] = keys.T
        keys_t_ref[block] = key_t
        values_ref[block] = value_t.T

    fill_keys(meta, own, others, groups, parts, docs, rows, store)
    accum_ref[...] = jnp.zeros_like(accum_ref)
    for j in range(groups):
        queries_ref[j] = query_full(meta, own[j][0, 0], j, groups, parts, docs, rows)
        grads_ref[j] = grads[j][0]

    def one_slot(j, carry):
        at = pl.ds(pl.multiple_of(j * rows, rows), rows)
        full = queries_ref[j]
        grad_t = grads_ref[j]
        delta = jnp.sum(grad_t.astype(jnp.float32) * wide_ref[0, :, at], axis=0, keepdims=True)
        log_total = log_ref[0, :, at]
        blank = jnp.zeros((HD, rows), jnp.bfloat16)
        both = jnp.concatenate(
            [
                jnp.concatenate([full[:HD], blank], axis=1),
                jnp.concatenate([blank, grad_t], axis=1),
            ],
            axis=0,
        )

        def step(t, grad_query):
            scores = dot(keys_ref[t], full)
            probs = jnp.exp2(scores * coeff - log_total)
            d_probs = dot(values_ref[t], grad_t)
            d_scores = (probs * (d_probs - delta)).astype(jnp.bfloat16)
            joined = jnp.concatenate([d_scores, probs.astype(jnp.bfloat16)], axis=1)
            accum_ref[t] += dot_t(joined, both)
            return grad_query + dot(keys_t_ref[t], d_scores)

        grad_query = lax.fori_loop(
            meta[2 + docs + 2 * j],
            meta[3 + docs + 2 * j],
            step,
            jnp.zeros((HD, rows), jnp.float32),
        )
        dq_ref[:, at] = (grad_query * HD**-0.5).astype(jnp.bfloat16)
        return carry

    lax.fori_loop(0, groups, one_slot, 0)
    g, s = meta[0], meta[1]
    for j in range(groups):
        for e in range(parts):
            block = lax.rem(g - j + groups, groups) * parts + lax.rem(s - e + parts, parts)
            terms = accum_ref[block].T
            at = slice(j * rows, (j + 1) * rows)
            d_key = terms[:HD] * HD**-0.5
            d_value = terms[HD:]
            if e == 0:
                mine_ref[0, :, at] = d_key
                mine_ref[1, :, at] = d_value
            else:
                theirs[e - 1, 0, :, at] = d_key.astype(jnp.bfloat16)
                theirs[e - 1, 1, :, at] = d_value.astype(jnp.bfloat16)


def head_block(head, *shape):
    dims = tuple(1 if n is None else n for n in shape)
    where = shape.index(None)

    def at(h, meta):
        chosen = h if head is None else head
        return tuple(chosen if i == where else 0 for i in range(len(dims)))

    return pl.BlockSpec(dims, at)


def attend(meta, own, others, groups, parts, docs, rows, heads):
    tiles = groups * parts
    tokens = groups * rows
    block = partial(head_block, None)
    grid_spec = pltpu.PrefetchScalarGridSpec(
        num_scalar_prefetch=1,
        grid=(heads,),
        in_specs=[block(3, None, HD, rows)] * groups
        + [block(2, None, HD, rows)] * (groups * (parts - 1)),
        out_specs=[block(None, HD, tokens), block(None, HD, tokens), block(None, 1, tokens)],
        scratch_shapes=[
            pltpu.VMEM((groups, 2 * HD, rows), jnp.bfloat16),
            pltpu.VMEM((tiles, rows, 2 * HD), jnp.bfloat16),
            pltpu.VMEM((tiles, HD, rows), jnp.bfloat16),
        ],
    )
    return pl.pallas_call(
        partial(attend_kernel, groups, parts, docs, rows),
        grid_spec=grid_spec,
        out_shape=[
            jax.ShapeDtypeStruct((heads, HD, tokens), jnp.bfloat16),
            jax.ShapeDtypeStruct((heads, HD, tokens), jnp.float32),
            jax.ShapeDtypeStruct((heads, 1, tokens), jnp.float32),
        ],
        cost_estimate=pl.CostEstimate(
            flops=KERNEL_FLOPS * 2 * heads,
            transcendentals=0,
            bytes_accessed=KERNEL_BYTES * heads,
        ),
        name="attend",
    )(meta, *own, *others)


def attend_back(head, meta, own, others, grads, wide, log_total, groups, parts, docs, rows):
    tiles = groups * parts
    tokens = groups * rows
    block = partial(head_block, head)
    plain = lambda *dims: pl.BlockSpec(dims, lambda h, meta: (0,) * len(dims))
    out_specs = [plain(HD, tokens), plain(2, HD, tokens)]
    out_shape = [
        jax.ShapeDtypeStruct((HD, tokens), jnp.bfloat16),
        jax.ShapeDtypeStruct((2, HD, tokens), jnp.float32),
    ]
    if parts > 1:
        out_specs.append(plain(parts - 1, 2, HD, tokens))
        out_shape.append(jax.ShapeDtypeStruct((parts - 1, 2, HD, tokens), jnp.bfloat16))
    grid_spec = pltpu.PrefetchScalarGridSpec(
        num_scalar_prefetch=1,
        grid=(1,),
        in_specs=[block(3, None, HD, rows)] * groups
        + [block(2, None, HD, rows)] * (groups * (parts - 1))
        + [block(None, HD, rows)] * groups
        + [block(None, HD, tokens), block(None, 1, tokens)],
        out_specs=out_specs,
        scratch_shapes=[
            pltpu.VMEM((groups, 2 * HD, rows), jnp.bfloat16),
            pltpu.VMEM((groups, HD, rows), jnp.bfloat16),
            pltpu.VMEM((tiles, rows, 2 * HD), jnp.bfloat16),
            pltpu.VMEM((tiles, HD, rows), jnp.bfloat16),
            pltpu.VMEM((tiles, rows, HD), jnp.bfloat16),
            pltpu.VMEM((tiles, rows, 2 * HD), jnp.float32),
        ],
    )
    return pl.pallas_call(
        partial(attend_back_kernel, groups, parts, docs, rows),
        grid_spec=grid_spec,
        out_shape=out_shape,
        cost_estimate=pl.CostEstimate(
            flops=KERNEL_FLOPS * 5, transcendentals=0, bytes_accessed=KERNEL_BYTES
        ),
        name="attend_back",
    )(meta, *own, *others, *grads, wide, log_total)


ERFC = (
    -1.26551223, 1.00002368, 0.37409196, 0.09678418, -0.18628806,
    0.27886807, -1.13520398, 1.48851587, -0.82215223, 0.17087277,
)


def normal_terms(v):
    z = jnp.abs(v) * (0.5**0.5)
    t = 1.0 / (1.0 + 0.5 * z)
    poly = jnp.full_like(t, ERFC[-1])
    for term in reversed(ERFC[:-1]):
        poly = poly * t + term
    square = z * z
    tail = 0.5 * t * jnp.exp(poly - square)
    below = jnp.where(v < 0, tail, 1.0 - tail)
    return below, jnp.exp(-square) * (2.0 * math.pi) ** -0.5


def normed(resid):
    centred = resid - jnp.mean(resid, axis=-1, keepdims=True)
    spread = jnp.mean(centred * centred, axis=-1, keepdims=True)
    scale = lax.rsqrt(spread + EPSILON)
    return centred * scale, scale


def norm_back(grad, gain, unit, scale):
    e = grad * gain
    inner = jnp.mean(e * unit, axis=-1, keepdims=True)
    return (e - jnp.mean(e, axis=-1, keepdims=True) - unit * inner) * scale


def over_blocks(count, aligned, step, value):
    if aligned:
        return lax.fori_loop(0, count, step, value)
    for i in range(count):
        value = step(i, value)
    return value


def feed_kernel(
    tokens_ref,
    attended_ref,
    cot_ref,
    out_ref,
    in_ref,
    back_ref,
    vec_ref,
    in_bias_ref,
    result_ref,
    d_resid1_ref,
    d_attended_ref,
    hidden_ref,
    act_ref,
    d_ffn_ref,
    d_pre_ref,
    d_branch_ref,
    sums_ref,
    in_sums_ref,
    slope_ref,
):
    f32, bf16 = jnp.float32, jnp.bfloat16
    out_shift, gain_one, shift_one = vec_ref[0:1], vec_ref[1:2], vec_ref[2:3]
    back_shift, gain_two, shift_two = vec_ref[3:4], vec_ref[4:5], vec_ref[5:6]

    @pl.when(pl.program_id(0) == 0)
    def _():
        sums_ref[...] = jnp.zeros_like(sums_ref)
        in_sums_ref[...] = jnp.zeros_like(in_sums_ref)

    total = lambda a: jnp.sum(a, axis=0, keepdims=True)
    branch = dot(attended_ref[...].T, out_ref[...]) + out_shift
    unit1, scale1 = normed(tokens_ref[...].astype(f32) + branch)
    hidden = unit1 * gain_one + shift_one
    hidden_low = hidden.astype(bf16)
    count, unused, shard = hidden_ref.shape
    for i in range(count):
        hidden_ref[i] = hidden_low[:, i * shard : (i + 1) * shard]
    resid2 = hidden + back_shift
    blocks, unused, size = act_ref.shape
    aligned = size % 128 == 0
    columns = lambda i: pl.ds(pl.multiple_of(i * size, size) if aligned else i * size, size)

    def forward(i, resid2):
        cols = columns(i)
        pre = dot(hidden_low, in_ref[:, cols]) + in_bias_ref[:, cols]
        below, density = normal_terms(pre)
        act = (pre * below).astype(bf16)
        act_ref[i] = act
        slope_ref[i] = below + pre * density
        return resid2 + dot(act, back_ref[cols, :])

    resid2 = over_blocks(blocks, aligned, forward, hidden + back_shift)
    unit2, scale2 = normed(resid2)
    result_ref[...] = (unit2 * gain_two + shift_two).astype(bf16)
    cot = cot_ref[...].astype(f32)
    d_resid2 = norm_back(cot, gain_two, unit2, scale2)
    d_ffn = d_resid2.astype(bf16)
    d_ffn_ref[...] = d_ffn

    def backward(i, d_hidden):
        cols = columns(i)
        d_act = dot_t(d_ffn, back_ref[cols, :])
        d_pre = (d_act * slope_ref[i]).astype(bf16)
        d_pre_ref[:, cols] = d_pre
        in_sums_ref[:, cols] += total(d_pre.astype(f32))
        return d_hidden + dot_t(d_pre, in_ref[:, cols])

    d_hidden = over_blocks(blocks, aligned, backward, d_resid2)
    d_resid1 = norm_back(d_hidden, gain_one, unit1, scale1)
    d_resid1_ref[...] = d_resid1
    d_branch = d_resid1.astype(bf16)
    d_branch_ref[...] = d_branch
    d_attended_ref[...] = dot_t(out_ref[...], d_branch).astype(bf16)
    sums_ref[...] += jnp.concatenate(
        [
            total(d_branch.astype(f32)),
            total(d_hidden * unit1),
            total(d_hidden),
            total(d_ffn.astype(f32)),
            total(cot * unit2),
            total(cot),
            jnp.zeros((2, cot.shape[1]), f32),
        ],
        axis=0,
    )


def feed_forward(fsdp, tokens, attended_t, cotangent, out_full, in_full, back_full, vectors, in_shift):
    f32, bf16 = jnp.float32, jnp.bfloat16
    rows, model = tokens.shape
    inner = in_full.shape[1]
    tile = math.gcd(rows, 256)
    by_rows = lambda n: pl.BlockSpec((tile, n), lambda i: (i, 0))
    by_cols = lambda n: pl.BlockSpec((n, tile), lambda i: (0, i))
    blocks = lambda n: pl.BlockSpec((fsdp, tile, n // fsdp), lambda i: (0, i, 0))
    fixed = lambda m, n: pl.BlockSpec((m, n), lambda i: (0, 0))
    shape = jax.ShapeDtypeStruct
    return pl.pallas_call(
        feed_kernel,
        grid=(rows // tile,),
        in_specs=[
            by_rows(model), by_cols(model), by_rows(model), fixed(model, model),
            fixed(model, inner), fixed(inner, model), fixed(8, model), fixed(1, inner),
        ],
        out_specs=[
            by_rows(model), by_rows(model), by_cols(model), blocks(model), blocks(inner),
            by_rows(model), by_rows(inner), by_rows(model), fixed(8, model), fixed(1, inner),
        ],
        out_shape=[
            shape((rows, model), bf16), shape((rows, model), f32), shape((model, rows), bf16),
            shape((fsdp, rows, model // fsdp), bf16), shape((fsdp, rows, inner // fsdp), bf16),
            shape((rows, model), bf16),
            shape((rows, inner), bf16), shape((rows, model), bf16), shape((8, model), f32),
            shape((1, inner), f32),
        ],
        scratch_shapes=[pltpu.VMEM((fsdp, tile, inner // fsdp), f32)],
        cost_estimate=pl.CostEstimate(
            flops=rows * model * (8 * inner + 4 * model), transcendentals=0, bytes_accessed=30_000_000
        ),
        name="feed_forward",
    )(tokens, attended_t, cotangent, out_full, in_full, back_full, vectors, in_shift)


def weight_grad_kernel(which, *refs):
    ins, (d_ffn, d_pre, d_branch), outs = refs[:8], refs[8:11], refs[11:]
    bf16 = jnp.bfloat16
    for side in range(2):
        act, hidden, attended_t, line = ins[4 * side : 4 * side + 4]
        lower, upper = outs[2 * side : 2 * side + 2]
        first, second = act.shape[2], attended_t.shape[0]
        lower[0, :first] = dot(act[0].T, d_ffn[...]).astype(bf16)
        lower[0, first : first + second] = dot(attended_t[...], d_branch[...]).astype(bf16)
        lower[0, first + second :] = line[0].astype(bf16)
        upper[0] = dot(hidden[0].T, d_pre[...]).astype(bf16)


def weight_grads(which, act, hidden, attended_t, line, d_ffn, d_pre, d_branch):
    fsdp, rows, inner_shard = act.shape
    shard = hidden.shape[2]
    model, inner = d_ffn.shape[1], d_pre.shape[1]
    line_rows = line.shape[1]
    tall = inner_shard + shard + line_rows
    half = fsdp // 2
    in_specs = []
    for side in range(2):
        block = lambda i, w, side=side: 2 * i + w[side]
        in_specs += [
            pl.BlockSpec((1, rows, inner_shard), lambda i, w, b=block: (b(i, w), 0, 0)),
            pl.BlockSpec((1, rows, shard), lambda i, w, b=block: (b(i, w), 0, 0)),
            pl.BlockSpec((shard, rows), lambda i, w, b=block: (b(i, w), 0)),
            pl.BlockSpec((1, line_rows, model), lambda i, w, b=block: (b(i, w), 0, 0)),
        ]
    in_specs += [pl.BlockSpec((rows, n), lambda i, w: (0, 0)) for n in (model, inner, model)]
    out = [(tall, model), (shard, inner)] * 2
    return pl.pallas_call(
        weight_grad_kernel,
        grid_spec=pltpu.PrefetchScalarGridSpec(
            num_scalar_prefetch=1,
            grid=(half,),
            in_specs=in_specs,
            out_specs=[pl.BlockSpec((1,) + o, lambda i, w: (i, 0, 0)) for o in out],
        ),
        out_shape=[jax.ShapeDtypeStruct((half,) + o, jnp.bfloat16) for o in out],
        cost_estimate=pl.CostEstimate(
            flops=2 * rows * model * (2 * inner + model), transcendentals=0, bytes_accessed=25_000_000
        ),
        name="weight_grads",
    )(which, act, hidden, attended_t, line, act, hidden, attended_t, line, d_ffn, d_pre, d_branch)


def qkv_grad_kernel(fsdp, which, *refs):
    slots, (d_qkv, send, keep, total) = refs[:-4], refs[-4:]
    rows = slots[0].shape[0]
    shard = send.shape[1] - PAD
    value = None
    for j, slot in enumerate(slots):
        term = dot_t(slot[...].T, d_qkv[:, j * rows : (j + 1) * rows])
        value = term if value is None else value + term
    total[...] = value
    ones = jnp.ones((PAD, d_qkv.shape[1]), jnp.bfloat16)
    sums = dot_t(ones, d_qkv[...]).astype(jnp.bfloat16)
    for side, ref in enumerate((send, keep)):
        for i in range(fsdp // 2):
            at = pl.multiple_of((2 * i + which[side]) * shard, math.gcd(shard, 64))
            ref[i, :shard] = total[pl.ds(at, shard), :].astype(jnp.bfloat16)
            ref[i, shard:] = sums


def qkv_grads(which, slots, d_qkv_t, fsdp):
    rows, model = slots[0].shape
    width = d_qkv_t.shape[0]
    out = (fsdp // 2, model // fsdp + PAD, width)
    fixed = lambda dims: pl.BlockSpec(dims, lambda i, w: (0,) * len(dims))
    return pl.pallas_call(
        partial(qkv_grad_kernel, fsdp),
        grid_spec=pltpu.PrefetchScalarGridSpec(
            num_scalar_prefetch=1,
            grid=(1,),
            in_specs=[fixed((rows, model))] * len(slots) + [fixed(d_qkv_t.shape)],
            out_specs=[fixed(out)] * 2,
            scratch_shapes=[pltpu.VMEM((model, width), jnp.float32)],
        ),
        out_shape=[jax.ShapeDtypeStruct(out, jnp.bfloat16)] * 2,
        cost_estimate=pl.CostEstimate(
            flops=2 * rows * len(slots) * model * width, transcendentals=0, bytes_accessed=8_000_000
        ),
        name="qkv_grads",
    )(which, *slots, d_qkv_t)


def body(
    inputs,
    doc_starts,
    qkv_weight,
    query_bias,
    value_bias,
    out_weight,
    out_bias,
    norm1_gain,
    norm1_bias,
    in_weight,
    in_bias,
    back_weight,
    back_bias,
    norm2_gain,
    norm2_bias,
    cotangent,
):
    bf16, f32 = jnp.bfloat16, jnp.float32
    tokens = inputs[0]
    rows, model = tokens.shape
    starts = doc_starts[0]
    docs = starts.shape[0]
    ctx = lax.axis_size("ctx")
    fsdp = lax.axis_size("fsdp")
    groups = math.gcd(H, ctx)
    parts = ctx // groups
    heads = H // groups
    span = heads * HD
    width = 3 * span
    index = lax.axis_index("ctx")
    g, s = index // parts, index % parts
    f = lax.axis_index("fsdp")
    shard = model // fsdp

    slots = [tokens] + [ctx_shift(tokens, groups, parts, d, 0) for d in range(1, groups)]

    own_cols = pick(qkv_weight.reshape(shard, 3, groups, span), g, 2).reshape(shard, width)
    small = jnp.concatenate(
        [
            query_bias, value_bias, out_bias, norm1_gain, norm1_bias,
            back_bias, norm2_gain, norm2_bias, in_bias,
        ]
    )
    count = small.shape[0]
    extra = -(-count // (width * PAD)) * PAD
    small_block = jnp.pad(small, (0, extra * width - count)).reshape(extra, width)
    first = jnp.concatenate([own_cols, small_block], axis=0)
    first_top = gather_top(first)
    first_top, out_held, in_held, back_held = together(
        first_top, out_weight, in_weight, back_weight
    )
    out_top, in_top, back_top = gather_top(out_held), gather_top(in_held), gather_top(back_held)
    first = gather_rest(first, first_top)
    own_weight = first[:, :shard].reshape(model, width)
    flat = first[:, shard:].reshape(fsdp, extra * width)[:, :count].astype(f32)
    vector = lambda i: flat[:, i * shard : (i + 1) * shard].reshape(model)
    query_shift, value_shift = vector(0), vector(1)
    vectors = jnp.pad(jnp.stack([vector(i) for i in range(2, 8)]), ((0, 2), (0, 0)))
    in_shift = flat[:, 8 * shard :].reshape(1, -1)

    zero = jnp.zeros((span,), f32)
    own_shift = jnp.concatenate(
        [
            lax.dynamic_slice(query_shift, (g * span,), (span,)),
            zero,
            lax.dynamic_slice(value_shift, (g * span,), (span,)),
        ]
    )
    own, others = [], []
    for slot in slots:
        projected = lax.dot_general(
            own_weight, slot, (((0,), (1,)), ((), ())), preferred_element_type=f32
        )
        low = (projected + own_shift[:, None]).astype(bf16).reshape(3, heads, HD, rows)
        own.append(low)
    for e in range(1, parts):
        for low in own:
            others.append(ctx_shift(low[1:], groups, parts, 0, e))
    if parts > 1:
        in_top, others[0], others[1] = together(in_top, others[0], others[1])

    bounds = jnp.concatenate([starts, jnp.full((1,), ctx * rows, jnp.int32)])
    base = ((g - jnp.arange(groups, dtype=jnp.int32) + groups) % groups) * parts + s
    heads_at = base * rows
    tails_at = heads_at + rows - 1
    low_edge = jnp.max(jnp.where(starts[None] <= heads_at[:, None], starts[None], 0), axis=1)
    high_edge = jnp.min(
        jnp.where(bounds[None] > tails_at[:, None], bounds[None], ctx * rows), axis=1
    )
    ranges = jnp.stack([low_edge // rows, (high_edge + rows - 1) // rows], axis=1).reshape(-1)
    meta = jnp.concatenate([jnp.stack([g, s]).astype(jnp.int32), starts, ranges.astype(jnp.int32)])

    out_full = gather_rest(out_weight, out_top).reshape(model, model)
    in_full = gather_rest(in_weight, in_top).reshape(model, -1)
    meta, out_full, in_full = together(meta, out_full, in_full)
    low, wide, log_total = attend(meta, own, others, groups, parts, docs, rows, heads)
    low, qkv_held = together(low, qkv_weight)
    attended_t = jnp.zeros((groups * span, rows), bf16)
    turned = []
    for j in range(groups):
        piece = low[:, :, j * rows : (j + 1) * rows]
        turned.append(ctx_shift(piece, groups, parts, -j, 0) if j else piece)
    for j, piece in enumerate(together(*turned)):
        attended_t = lax.dynamic_update_slice(
            attended_t, piece.reshape(span, rows), (((g + j) % groups) * span, 0)
        )
    back_full = gather_rest(back_weight, back_top).reshape(-1, model)

    (
        result, d_resid1, d_attended_t, hidden_low, act_low, d_ffn_low, d_pre_low, d_branch_low,
        sums, in_sums,
    ) = feed_forward(
        fsdp, tokens, attended_t, cotangent[0], out_full, in_full, back_full, vectors, in_shift
    )
    grads = []
    for j in range(groups):
        part = lax.dynamic_slice(d_attended_t, (((g + j) % groups) * span, 0), (span, rows))
        part = part.reshape(heads, HD, rows)
        grads.append(ctx_shift(part, groups, parts, j, 0) if j else part)

    inner = in_full.shape[1]
    inner_shard = in_bias.shape[0]
    line = jnp.concatenate(
        [sums[:6].reshape(6, fsdp, shard).transpose(1, 0, 2).reshape(fsdp, -1), in_sums.reshape(fsdp, -1)],
        axis=1,
    )
    line_rows = -(inner_shard + shard) % 64 or 64
    line = jnp.pad(line, ((0, 0), (0, line_rows * model - line.shape[1])))
    line = line.reshape(fsdp, line_rows, model)
    mine = bit_at("fsdp", 0)
    which = jnp.stack([1 - mine, mine]).astype(jnp.int32)
    lower_send, upper_send, lower, upper = weight_grads(
        which, act_low, hidden_low, attended_t, line, d_ffn_low, d_pre_low, d_branch_low
    )
    lower = add_low(lower, swap(lower_send, "fsdp", 0))
    upper = add_low(upper, swap(upper_send, "fsdp", 0))
    fsdp_bits, ctx_bits = range(bits_of("fsdp")), range(bits_of("ctx"))
    chunks = inner // (2 * model)

    def pair_step(i, state):
        lower, upper = state
        lower_steps = [("fsdp", b) for b in fsdp_bits[1:]] + [("ctx", 0)]
        upper_steps = [("ctx", 0)] + [("fsdp", b) for b in fsdp_bits[1:]]
        return halve(lower, *lower_steps[i], 1), halve(upper, *upper_steps[i], 2)

    def merge(state):
        lower, upper = state
        return (
            jnp.concatenate(
                [lower[0]] + [upper[0, :, c * model : (c + 1) * model] for c in range(chunks)], axis=0
            ),
        )

    steps = [partial(pair_step, i) for i in range(len(fsdp_bits))]
    last = steps.pop()
    steps.append(lambda state: merge(last(state)))
    for bit in ctx_bits[1:-1]:
        steps.append(lambda state, bit=bit: (halve(state[0], "ctx", bit, 0),))
    state = (lower, upper)

    pieces, received = [], [[] for unused in range(groups)]
    held, theirs = None, None

    def send(piece):
        pieces.append(piece)
        for j in range(groups):
            part = piece[:, :, j * rows : (j + 1) * rows]
            received[j].append(ctx_shift(part, groups, parts, -j, 0) if j else part)

    def settle(dq, dkv, theirs):
        for other in theirs:
            dkv = dkv + other.astype(f32)
        send(jnp.concatenate([dq[None], dkv.astype(bf16)], axis=0))

    for head in range(heads):
        if head and steps:
            state = steps.pop(0)(state)
        meta, *state = together(meta, *state)
        dq, dkv, *rest = attend_back(
            head, meta, own, others, grads, wide, log_total, groups, parts, docs, rows
        )
        if head:
            dq, *theirs = together(dq, *theirs)
            settle(*held, theirs)
        held = (dq, dkv)
        theirs = [ctx_shift(rest[0][e - 1], groups, parts, 0, -e) for e in range(1, parts)]
    settle(*held, theirs)
    qkv_top = gather_top(qkv_held)
    qkv_full = gather_rest(qkv_held, qkv_top).reshape(model, 3 * model)
    for advance in steps:
        state = advance(state)
    merged = exchange(state[0], "ctx", ctx_bits[-1])
    for bit in reversed(ctx_bits[1:-1]):
        merged = double(merged, "ctx", bit, 0)
    other = swap(merged, "ctx", 0)
    lower_rows = (inner_shard + shard + line_rows) // 2
    lower = join(bit_at("ctx", 0), merged[:lower_rows], other[:lower_rows], 0)
    wide_half = lambda m: jnp.concatenate(
        [m[lower_rows + c * shard : lower_rows + (c + 1) * shard] for c in range(chunks)], axis=1
    )
    upper = join(bit_at("ctx", 0), wide_half(merged), wide_half(other), 1)

    d_qkv_t = jnp.stack(pieces, axis=1).reshape(width, groups * rows)
    qkv_send, qkv_sum = qkv_grads(which, slots, d_qkv_t, fsdp)
    qkv_sum = add_low(qkv_sum, swap(qkv_send, "fsdp", 0))
    for bit in fsdp_bits[1:]:
        qkv_sum = halve(qkv_sum, "fsdp", bit, 1)
    qkv_sum = qkv_sum[0]
    wide_sum = qkv_sum.astype(f32)
    for e in range(1, parts):
        wide_sum = wide_sum + ctx_shift(qkv_sum, groups, parts, 0, e).astype(f32)
    qkv_low = wide_sum.astype(bf16)
    flat = [part for parts_of in received for part in parts_of]
    qkv_low, *flat = together(qkv_low, *flat)
    received = [flat[j * heads : (j + 1) * heads] for j in range(groups)]
    by_group = jnp.zeros((groups,) + qkv_low.shape, bf16)
    for j in range(groups):
        piece = ctx_shift(qkv_low, groups, parts, -j, 0) if j else qkv_low
        by_group = lax.dynamic_update_slice(by_group, piece[None], ((g + j) % groups, 0, 0))
    natural = by_group.reshape(groups, shard + PAD, 3, span).transpose(1, 2, 0, 3)
    natural = natural.reshape(shard + PAD, 3 * model).astype(f32)
    grad_qkv_shard = natural[:shard]
    bias_line = natural[shard]
    grad_query_shift = lax.dynamic_slice(bias_line, (f * shard,), (shard,))
    grad_value_shift = lax.dynamic_slice(bias_line, (2 * model + f * shard,), (shard,))

    natural = jnp.zeros((3, groups, heads, HD, rows), bf16)
    for j in range(groups):
        part = jnp.stack(received[j], axis=1)[:, None]
        natural = lax.dynamic_update_slice(natural, part, (0, (g + j) % groups, 0, 0, 0))
    input_grad = d_resid1 + lax.dot_general(
        natural.reshape(3 * model, rows),
        qkv_full,
        (((0,), (1,)), ((), ())),
        preferred_element_type=f32,
    )

    ends = inner_shard + shard
    flat = lower[ends:].reshape(-1).astype(f32)
    offsets = lambda i: flat[i * shard : (i + 1) * shard]
    return (
        result[None],
        input_grad[None],
        grad_qkv_shard,
        grad_query_shift,
        grad_value_shift,
        lower[inner_shard:ends].astype(f32),
        offsets(0),
        offsets(1),
        offsets(2),
        upper.astype(f32),
        flat[6 * shard : 6 * shard + inner_shard],
        lower[:inner_shard].astype(f32),
        offsets(3),
        offsets(4),
        offsets(5),
    )


def solution(mesh):
    rows, one = P("fsdp", None), P("fsdp")
    whole = P("fsdp", "ctx", None)
    return jax.shard_map(
        body,
        mesh=mesh,
        in_specs=(
            whole, rows, rows, one, one, rows, one, one, one, rows, one, rows, one, one, one, whole,
        ),
        out_specs=(
            whole, whole, rows, one, one, rows, one, one, one, rows, one, rows, one, one, one,
        ),
        check_vma=False,
    )
```

profile of v0, /device:TPU:28, one launch (start us, length us, event | category | flops | bytes accessed | tf_op | source)
XLA Modules:
  0.0 509.6 jit_solution(7883935031509156615)
XLA Ops:
  9.0 5.6 %collective-permute-done = bf16[208,576]{0,1:T(8,128)(2,1)S(1)} collective-permute-done((bf16[208,576]{0,1:T(8,128)(2,1)S(1)}, bf16[208,576]{0,1:T(8,128)(2,1)S(1)}, u32[]{:S(2)}, u32[]{:S(2)}) %collective-permute-start) | collective-permute-done | bytes 239648 | tf_op jit(solution)/shard_map/ppermute | solution.py:31
  35.7 7.9 %collective-permute-done.5.refs_4_ = bf16[2,3,64,512]{3,2,1,0:T(8,128)(2,1)S(1)} collective-permute-done((bf16[2,3,64,512]{3,2,1,0:T(8,128)(2,1)S(1)}, bf16[2,3,64,512]{3,2,1,0:T(8,128)(2,1)S(1)}, u32[]{:S(2)}, u32[]{:S(2)}) %collective-permute-start.5) | collective-permute-done | bytes 393248 | tf_op jit(solution)/shard_map/ppermute | solution.py:26
  45.2 6.2 %collective-permute-done.7.refs_5_ = bf16[2,3,64,512]{3,2,1,0:T(8,128)(2,1)S(1)} collective-permute-done((bf16[2,3,64,512]{3,2,1,0:T(8,128)(2,1)S(1)}, bf16[2,3,64,512]{3,2,1,0:T(8,128)(2,1)S(1)}, u32[]{:S(2)}, u32[]{:S(2)}) %collective-permute-start.7) | collective-permute-done | bytes 393248 | tf_op jit(solution)/shard_map/ppermute | solution.py:26
  97.3 30.5 %attend.1 = (bf16[3,64,2048]{2,1,0:T(8,128)(2,1)}, f32[3,64,2048]{2,1,0:T(8,128)}, f32[3,1,2048]{2,1,0:T(1,128)}) custom-call(s32[18]{0:T(128)} %pad_add_fusion.2.meta, bf16[3,3,64,512]{3,2,1,0:T(8,128)(2,1)} %bitcast.210, bf16[3,3,64,512]{3,2,1,0:T(8,128)(2,1)} %bitcast.214, bf16[3,3,64,512]{3,2,1,0:T(8,128)(2,1)} %bitcast.218, ...), custom_call_target="tpu_custom_call" | custom-call | flops 17999998976 | bytes 60000000 | tf_op jit(solution)/shard_map/attend/pallas_call | solution.py:282
  129.1 17.7 %collective-permute-start.13 = (bf16[3,64,512]{2,1,0:T(8,128)(2,1)S(1)}, bf16[3,64,512]{2,1,0:T(8,128)(2,1)S(1)}, u32[]{:S(2)}, u32[]{:S(2)}) collective-permute-start(bf16[3,64,512]{2,1,0:T(8,128)(2,1)S(1)} %get-tuple-element.177), channel_id=1, source_target_pairs={{0,24},{4,28},{8,0},{12,4},{16,8},{20,12},{24,16},{28,20},{1,25},{... | collective-permute-start | bytes 589832 | tf_op jit(solution)/shard_map/ppermute | solution.py:26
  156.4 34.6 %feed_forward.1 = (bf16[512,768]{1,0:T(8,128)(2,1)}, f32[512,768]{1,0:T(8,128)}, bf16[768,512]{1,0:T(8,128)(2,1)}, bf16[4,512,192]{2,1,0:T(8,128)(2,1)}, bf16[4,...) custom-call(bf16[512,768]{1,0:T(8,128)(2,1)} %bitcast.tokens_ref.ref, ...), custom_call_target="tpu_custom_call" | custom-call | flops 10871635968 | bytes 30000000 | tf_op jit(solution)/shard_map/feed_forward/pallas_call | solution.py:477
  195.0 12.2 %weight_grads.1 = (bf16[2,1024,768]{2,1,0:T(8,128)(2,1)}, bf16[2,192,3072]{2,1,0:T(8,128)(2,1)}, bf16[2,1024,768]{2,1,0:T(8,128)(2,1)}, bf16[2,192,3072]{2,1,0:T(8,128)(2,1)}) custom-call(s32[2]{0:T(128)} %pad_add_fusion.3.which, bf16[4,512,768]{2,1,0:T(8,128)(2,1)} %get-tuple-element.102.refs_0_.refs_4_, ...), custom_call_target="tpu_custom_call" | custom-call | flops 5435817984 | bytes 25000000 | tf_op jit(solution)/shard_map/weight_grads/pallas_call | solution.py:534
  207.2 5.9 %collective-permute-start.19 = (bf16[2,192,3072]{2,1,0:T(8,128)(2,1)}, bf16[2,192,3072]{2,1,0:T(8,128)(2,1)}, u32[]{:S(2)}, u32[]{:S(2)}) collective-permute-start(bf16[2,192,3072]{2,1,0:T(8,128)(2,1)} %get-tuple-element.112), channel_id=1, source_target_pairs={{0,1},{1,0},{2,3},{3,2},{4,5},{5,4},{6,7},{7,6},{8,9},{9,8},{10,11... | collective-permute-start | bytes 7077896 | tf_op jit(solution)/shard_map/ppermute | solution.py:31
  214.0 6.3 %collective-permute-start.20 = (bf16[3,64,512]{2,1,0:T(8,128)(2,1)S(1)}, bf16[3,64,512]{2,1,0:T(8,128)(2,1)S(1)}, u32[]{:S(2)}, u32[]{:S(2)}) collective-permute-start(bf16[3,64,512]{2,1,0:T(8,128)(2,1)S(1)} %bitcast.231), channel_id=1, source_target_pairs={{0,8},{4,12},{8,16},{12,20},{16,24},{20,28},{24,0},{28,4},{1,9},{5... | collective-permute-start | bytes 589832 | tf_op jit(solution)/shard_map/ppermute | solution.py:26
  220.3 15.0 %collective-permute-done.42 = bf16[192,2304]{1,0:T(8,128)(2,1)S(1)} collective-permute-done((bf16[192,2304]{1,0:T(8,128)(2,1)S(1)}, bf16[192,2304]{1,0:T(8,128)(2,1)S(1)}, u32[]{:S(2)}, u32[]{:S(2)}) %collective-permute-start.42) | collective-permute-done | bytes 884768 | tf_op jit(solution)/shard_map/ppermute | solution.py:31
  255.0 14.9 %attend_back.3 = (bf16[64,2048]{1,0:T(8,128)(2,1)}, f32[2,64,2048]{2,1,0:T(8,128)}, bf16[1,2,64,2048]{3,2,1,0:T(8,128)(2,1)}) custom-call(s32[18]{0:T(128)} %pad_add_fusion.2.meta, bf16[3,3,64,512]{3,2,1,0:T(8,128)(2,1)} %bitcast.211, bf16[3,3,64,512]{3,2,1,0:T(8,128)(2,1)} %bitcast.215, bf16[3,3,64,512]{3,2,1,0:T(8,128)(2,1)} %bitcast.219, ...), custom_call_target="tpu_custom_call" | custom-call | flops 15000000512 | bytes 20000000 | tf_op jit(solution)/shard_map/attend_back/pallas_call | solution.py:329
  270.0 9.4 %collective-permute-done.24 = bf16[2,192,1536]{2,1,0:T(8,128)(2,1)} collective-permute-done((bf16[2,192,1536]{2,1,0:T(8,128)(2,1)}, bf16[2,192,1536]{2,1,0:T(8,128)(2,1)}, u32[]{:S(2)}, u32[]{:S(2)}) %collective-permute-start.24) | collective-permute-done | bytes 1179680 | tf_op jit(solution)/shard_map/ppermute | solution.py:31
  281.3 7.7 %collective-permute-done.23 = bf16[1,1024,768]{2,1,0:T(8,128)(2,1)} collective-permute-done((bf16[1,1024,768]{2,1,0:T(8,128)(2,1)}, bf16[1,1024,768]{2,1,0:T(8,128)(2,1)}, u32[]{:S(2)}, u32[]{:S(2)}) %collective-permute-start.23) | collective-permute-done | bytes 1572896 | tf_op jit(solution)/shard_map/ppermute | solution.py:31
  294.5 14.8 %attend_back.4 = (bf16[64,2048]{1,0:T(8,128)(2,1)}, f32[2,64,2048]{2,1,0:T(8,128)}, bf16[1,2,64,2048]{3,2,1,0:T(8,128)(2,1)}) custom-call(s32[18]{0:T(128)} %pad_add_fusion.2.meta, bf16[3,3,64,512]{3,2,1,0:T(8,128)(2,1)} %bitcast.212, bf16[3,3,64,512]{3,2,1,0:T(8,128)(2,1)} %bitcast.216, bf16[3,3,64,512]{3,2,1,0:T(8,128)(2,1)} %bitcast.220, ...), custom_call_target="tpu_custom_call" | custom-call | flops 15000000512 | bytes 20000000 | tf_op jit(solution)/shard_map/attend_back/pallas_call | solution.py:329
  316.3 14.7 %attend_back.5 = (bf16[64,2048]{1,0:T(8,128)(2,1)}, f32[2,64,2048]{2,1,0:T(8,128)}, bf16[1,2,64,2048]{3,2,1,0:T(8,128)(2,1)}) custom-call(s32[18]{0:T(128)} %pad_add_fusion.2.meta, bf16[3,3,64,512]{3,2,1,0:T(8,128)(2,1)} %bitcast.213, bf16[3,3,64,512]{3,2,1,0:T(8,128)(2,1)} %bitcast.217, bf16[3,3,64,512]{3,2,1,0:T(8,128)(2,1)} %bitcast.221, ...), custom_call_target="tpu_custom_call" | custom-call | flops 15000000512 | bytes 20000000 | tf_op jit(solution)/shard_map/attend_back/pallas_call | solution.py:329
  332.8 13.3 %collective-permute-done.29 = bf16[2,64,2048]{2,1,0:T(8,128)(2,1)S(1)} collective-permute-done((bf16[2,64,2048]{2,1,0:T(8,128)(2,1)}, bf16[2,64,2048]{2,1,0:T(8,128)(2,1)S(1)}, u32[]{:S(2)}, u32[]{:S(2)}) %collective-permute-start.29) | collective-permute-done | bytes 524320 | tf_op jit(solution)/shard_map/ppermute | solution.py:26
  348.9 7.7 %qkv_grads.1 = (bf16[2,208,576]{2,1,0:T(8,128)(2,1)}, bf16[2,208,576]{2,1,0:T(8,128)(2,1)}) custom-call(s32[2]{0:T(128)} %pad_add_fusion.3.which, bf16[512,768]{1,0:T(8,128)(2,1)} %bitcast.tokens_ref.refs_0_, bf16[512,768]{1,0:T(8,128)(2,1)} %collective-permute-done.6.refs_1_, bf16[512,768]{1,0:T(8,128)(2,1)} %collective-permute-done.9.refs_2_, ...), custom_call_target="tpu_custom_call" | custom-call | flops 1811939328 | bytes 8000000 | tf_op jit(solution)/shard_map/qkv_grads/pallas_call | solution.py:573
  368.7 7.0 %collective-permute-done.31 = bf16[1,208,576]{2,1,0:T(8,128)(2,1)S(1)} collective-permute-done((bf16[1,208,576]{2,1,0:T(8,128)(2,1)S(1)}, bf16[1,208,576]{2,1,0:T(8,128)(2,1)S(1)}, u32[]{:S(2)}, u32[]{:S(2)}) %collective-permute-start.31) | collective-permute-done | bytes 239648 | tf_op jit(solution)/shard_map/ppermute | solution.py:31
  376.3 17.3 %collective-permute-start.37 = (bf16[3,64,512]{2,1,0:T(8,128)(2,1)S(1)}, bf16[3,64,512]{2,1,0:T(8,128)(2,1)S(1)}, u32[]{:S(2)}, u32[]{:S(2)}) collective-permute-start(bf16[3,64,512]{2,1,0:T(8,128)(2,1)S(1)} %get-tuple-element.166), channel_id=1, source_target_pairs={{0,16},{4,20},{8,24},{12,28},{16,0},{20,4},{24,8},{28,12},{1,17},{... | collective-permute-start | bytes 589832 | tf_op jit(solution)/shard_map/ppermute | solution.py:26
  393.6 26.4 %collective-permute-done.48 = bf16[448,768]{1,0:T(8,128)(2,1)S(1)} collective-permute-done((bf16[448,768]{1,0:T(8,128)(2,1)S(1)}, bf16[448,768]{1,0:T(8,128)(2,1)S(1)}, u32[]{:S(2)}, u32[]{:S(2)}) %collective-permute-start.48) | collective-permute-done | bytes 688160 | tf_op jit(solution)/shard_map/ppermute | solution.py:31
  424.3 5.9 %collective-permute-start.41 = (bf16[3,64,512]{2,1,0:T(8,128)(2,1)S(1)}, bf16[3,64,512]{2,1,0:T(8,128)(2,1)S(1)}, u32[]{:S(2)}, u32[]{:S(2)}) collective-permute-start(bf16[3,64,512]{2,1,0:T(8,128)(2,1)S(1)} %get-tuple-element.159), channel_id=1, source_target_pairs={{0,8},{4,12},{8,16},{12,20},{16,24},{20,28},{24,0},{28,4},{1,9},{5... | collective-permute-start | bytes 589832 | tf_op jit(solution)/shard_map/ppermute | solution.py:26
  432.7 8.4 %collective-permute-done.38 = bf16[3,64,512]{2,1,0:T(8,128)(2,1)S(1)} collective-permute-done((bf16[3,64,512]{2,1,0:T(8,128)(2,1)S(1)}, bf16[3,64,512]{2,1,0:T(8,128)(2,1)S(1)}, u32[]{:S(2)}, u32[]{:S(2)}) %collective-permute-start.38) | collective-permute-done | bytes 196640 | tf_op jit(solution)/shard_map/ppermute | solution.py:26
  448.8 18.4 %collective-permute-done.49 = bf16[448,768]{1,0:T(8,128)(2,1)S(1)} collective-permute-done((bf16[448,768]{1,0:T(8,128)(2,1)S(1)}, bf16[448,768]{1,0:T(8,128)(2,1)S(1)}, u32[]{:S(2)}, u32[]{:S(2)}) %collective-permute-start.49) | collective-permute-done | bytes 688160 | tf_op jit(solution)/shard_map/ppermute | solution.py:31
  485.0 16.0 %collective-permute-done.50 = bf16[896,768]{1,0:T(8,128)(2,1)} collective-permute-done((bf16[896,768]{1,0:T(8,128)(2,1)}, bf16[896,768]{1,0:T(8,128)(2,1)}, u32[]{:S(2)}, u32[]{:S(2)}) %collective-permute-start.50) | collective-permute-done | bytes 1376288 | tf_op jit(solution)/shard_map/ppermute | solution.py:31
  (362 shorter events, 183.7 us)
Async XLA Ops:
  6.3 69.8 %collective-permute-start.9 = (bf16[512,768]{1,0:T(8,128)(2,1)}, bf16[512,768]{1,0:T(8,128)(2,1)}, u32[]{:S(2)}, u32[]{:S(2)}) collective-permute-start(bf16[512,768]{1,0:T(8,128)(2,1)} %bitcast.tokens_ref.refs_0_), channel_id=1, source_target_pairs={{0,16},{4,20},{8,24},{12,28},{16,0},{20,4},{24,8},{28,12},{1,17},{... | collective-permute-start | bytes 2359304 | tf_op jit(solution)/shard_map/ppermute | solution.py:26
  8.2 71.7 %collective-permute-start.10 = (bf16[512,768]{1,0:T(8,128)(2,1)}, bf16[512,768]{1,0:T(8,128)(2,1)}, u32[]{:S(2)}, u32[]{:S(2)}) collective-permute-start(bf16[512,768]{1,0:T(8,128)(2,1)} %bitcast.tokens_ref.refs_0_), channel_id=1, source_target_pairs={{0,24},{4,28},{8,0},{12,4},{16,8},{20,12},{24,16},{28,20},{1,25},{... | collective-permute-start | bytes 2359304 | tf_op jit(solution)/shard_map/ppermute | solution.py:26
  17.4 33.9 %collective-permute-start.3 = (bf16[192,3072]{1,0:T(8,128)(2,1)S(1)}, bf16[192,3072]{1,0:T(8,128)(2,1)S(1)}, u32[]{:S(2)}, u32[]{:S(2)}) collective-permute-start(bf16[192,3072]{1,0:T(8,128)(2,1)S(1)} %copy-done.6), channel_id=1, source_target_pairs={{0,2},{1,3},{2,0},{3,1},{4,6},{5,7},{6,4},{7,5},{8,10},{9,11},{10,... | collective-permute-start | bytes 3538952 | tf_op jit(solution)/shard_map/ppermute | solution.py:31
  53.8 34.5 %collective-permute-start.8 = (bf16[2,192,3072]{2,1,0:T(8,128)(2,1)}, bf16[2,192,3072]{2,1,0:T(8,128)(2,1)}, u32[]{:S(2)}, u32[]{:S(2)}) collective-permute-start(bf16[2,192,3072]{2,1,0:T(8,128)(2,1)} %maximum_select_fusion.4), channel_id=1, source_target_pairs={{0,1},{1,0},{2,3},{3,2},{4,5},{5,4},{6,7},{7,6},{8,9},{9,8},{10,11... | collective-permute-start | bytes 7077896 | tf_op jit(solution)/shard_map/ppermute | solution.py:31
  55.2 28.6 %collective-permute-start.16 = (bf16[768,768]{1,0:T(8,128)(2,1)S(1)}, bf16[768,768]{1,0:T(8,128)(2,1)S(1)}, u32[]{:S(2)}, u32[]{:S(2)}) collective-permute-start(bf16[768,768]{1,0:T(8,128)(2,1)S(1)} %copy-done.5), channel_id=1, source_target_pairs={{0,2},{1,3},{2,0},{3,1},{4,6},{5,7},{6,4},{7,5},{8,10},{9,11},{10,... | collective-permute-start | bytes 3538952 | tf_op jit(solution)/shard_map/ppermute | solution.py:31
  85.6 64.1 %collective-permute-start.17 = (bf16[2,768,768]{2,1,0:T(8,128)(2,1)}, bf16[2,768,768]{2,1,0:T(8,128)(2,1)}, u32[]{:S(2)}, u32[]{:S(2)}) collective-permute-start(bf16[2,768,768]{2,1,0:T(8,128)(2,1)} %maximum_select_fusion.6), channel_id=1, source_target_pairs={{0,1},{1,0},{2,3},{3,2},{4,5},{5,4},{6,7},{7,6},{8,9},{9,8},{10,11... | collective-permute-start | bytes 7077896 | tf_op jit(solution)/shard_map/ppermute | solution.py:31
  207.2 34.7 %collective-permute-start.19 = (bf16[2,192,3072]{2,1,0:T(8,128)(2,1)}, bf16[2,192,3072]{2,1,0:T(8,128)(2,1)}, u32[]{:S(2)}, u32[]{:S(2)}) collective-permute-start(bf16[2,192,3072]{2,1,0:T(8,128)(2,1)} %get-tuple-element.112), channel_id=1, source_target_pairs={{0,1},{1,0},{2,3},{3,2},{4,5},{5,4},{6,7},{7,6},{8,9},{9,8},{10,11... | collective-permute-start | bytes 7077896 | tf_op jit(solution)/shard_map/ppermute | solution.py:31
  213.2 32.3 %collective-permute-start.18 = (bf16[2,1024,768]{2,1,0:T(8,128)(2,1)}, bf16[2,1024,768]{2,1,0:T(8,128)(2,1)}, u32[]{:S(2)}, u32[]{:S(2)}) collective-permute-start(bf16[2,1024,768]{2,1,0:T(8,128)(2,1)} %get-tuple-element.110), channel_id=1, source_target_pairs={{0,1},{1,0},{2,3},{3,2},{4,5},{5,4},{6,7},{7,6},{8,9},{9,8},{10,11... | collective-permute-start | bytes 9437192 | tf_op jit(solution)/shard_map/ppermute | solution.py:31
  214.0 38.9 %collective-permute-start.20 = (bf16[3,64,512]{2,1,0:T(8,128)(2,1)S(1)}, bf16[3,64,512]{2,1,0:T(8,128)(2,1)S(1)}, u32[]{:S(2)}, u32[]{:S(2)}) collective-permute-start(bf16[3,64,512]{2,1,0:T(8,128)(2,1)S(1)} %bitcast.231), channel_id=1, source_target_pairs={{0,8},{4,12},{8,16},{12,20},{16,24},{20,28},{24,0},{28,4},{1,9},{5... | collective-permute-start | bytes 589832 | tf_op jit(solution)/shard_map/ppermute | solution.py:26
  220.3 34.0 %collective-permute-start.21 = (bf16[3,64,512]{2,1,0:T(8,128)(2,1)S(1)}, bf16[3,64,512]{2,1,0:T(8,128)(2,1)S(1)}, u32[]{:S(2)}, u32[]{:S(2)}) collective-permute-start(bf16[3,64,512]{2,1,0:T(8,128)(2,1)S(1)} %bitcast.230), channel_id=1, source_target_pairs={{0,16},{4,20},{8,24},{12,28},{16,0},{20,4},{24,8},{28,12},{1,17},{... | collective-permute-start | bytes 589832 | tf_op jit(solution)/shard_map/ppermute | solution.py:26
  241.9 114.7 %collective-permute-start.43 = (bf16[2,192,2304]{2,1,0:T(8,128)(2,1)}, bf16[2,192,2304]{2,1,0:T(8,128)(2,1)}, u32[]{:S(2)}, u32[]{:S(2)}) collective-permute-start(bf16[2,192,2304]{2,1,0:T(8,128)(2,1)} %maximum_select_fusion.8), channel_id=1, source_target_pairs={{0,1},{1,0},{2,3},{3,2},{4,5},{5,4},{6,7},{7,6},{8,9},{9,8},{10,11... | collective-permute-start | bytes 5308424 | tf_op jit(solution)/shard_map/ppermute | solution.py:31
  250.2 29.2 %collective-permute-start.24 = (bf16[2,192,1536]{2,1,0:T(8,128)(2,1)}, bf16[2,192,1536]{2,1,0:T(8,128)(2,1)}, u32[]{:S(2)}, u32[]{:S(2)}) collective-permute-start(bf16[2,192,1536]{2,1,0:T(8,128)(2,1)} %constant_dynamic-slice_fusion.6), channel_id=1, source_target_pairs={{0,4},{4,0},{8,12},{12,8},{16,20},{20,16},{24,28},{28,24},{1,5},{5... | collective-permute-start | bytes 3538952 | tf_op jit(solution)/shard_map/ppermute | solution.py:31
  252.9 36.0 %collective-permute-start.23 = (bf16[1,1024,768]{2,1,0:T(8,128)(2,1)}, bf16[1,1024,768]{2,1,0:T(8,128)(2,1)}, u32[]{:S(2)}, u32[]{:S(2)}) collective-permute-start(bf16[1,1024,768]{2,1,0:T(8,128)(2,1)} %constant_dynamic-slice_fusion.7), channel_id=1, source_target_pairs={{0,2},{1,3},{2,0},{3,1},{4,6},{5,7},{6,4},{7,5},{8,10},{9,11},{10,... | collective-permute-start | bytes 4718600 | tf_op jit(solution)/shard_map/ppermute | solution.py:31
  270.0 41.1 %collective-permute-start.25 = (bf16[2,64,2048]{2,1,0:T(8,128)(2,1)}, bf16[2,64,2048]{2,1,0:T(8,128)(2,1)}, u32[]{:S(2)}, u32[]{:S(2)}) collective-permute-start(bf16[2,64,2048]{2,1,0:T(8,128)(2,1)} %bitcast.254), channel_id=1, source_target_pairs={{0,4},{4,0},{8,12},{12,8},{16,20},{20,16},{24,28},{28,24},{1,5},{5... | collective-permute-start | bytes 1572872 | tf_op jit(solution)/shard_map/ppermute | solution.py:26
  316.0 49.8 %collective-permute-start.47 = (bf16[448,768]{1,0:T(8,128)(2,1)}, bf16[448,768]{1,0:T(8,128)(2,1)}, u32[]{:S(2)}, u32[]{:S(2)}) collective-permute-start(bf16[448,768]{1,0:T(8,128)(2,1)} %constant_dynamic-slice_fusion), channel_id=1, source_target_pairs={{0,8},{4,12},{8,0},{12,4},{16,24},{20,28},{24,16},{28,20},{1,9},{5... | collective-permute-start | bytes 2064392 | tf_op jit(solution)/shard_map/ppermute | solution.py:31
  361.0 59.5 %collective-permute-start.36 = (bf16[3,64,512]{2,1,0:T(8,128)(2,1)S(1)}, bf16[3,64,512]{2,1,0:T(8,128)(2,1)S(1)}, u32[]{:S(2)}, u32[]{:S(2)}) collective-permute-start(bf16[3,64,512]{2,1,0:T(8,128)(2,1)S(1)} %get-tuple-element.170), channel_id=1, source_target_pairs={{0,16},{4,20},{8,24},{12,28},{16,0},{20,4},{24,8},{28,12},{1,17},{... | collective-permute-start | bytes 589832 | tf_op jit(solution)/shard_map/ppermute | solution.py:26
  364.4 56.2 %collective-permute-start.39 = (bf16[3,64,512]{2,1,0:T(8,128)(2,1)S(1)}, bf16[3,64,512]{2,1,0:T(8,128)(2,1)S(1)}, u32[]{:S(2)}, u32[]{:S(2)}) collective-permute-start(bf16[3,64,512]{2,1,0:T(8,128)(2,1)S(1)} %get-tuple-element.167), channel_id=1, source_target_pairs={{0,8},{4,12},{8,16},{12,20},{16,24},{20,28},{24,0},{28,4},{1,9},{5... | collective-permute-start | bytes 589832 | tf_op jit(solution)/shard_map/ppermute | solution.py:26
  367.0 53.0 %collective-permute-start.48 = (bf16[448,768]{1,0:T(8,128)(2,1)S(1)}, bf16[448,768]{1,0:T(8,128)(2,1)S(1)}, u32[]{:S(2)}, u32[]{:S(2)}) collective-permute-start(bf16[448,768]{1,0:T(8,128)(2,1)S(1)} %add_convert_fusion.6), channel_id=1, source_target_pairs={{0,16},{4,20},{8,24},{12,28},{16,0},{20,4},{24,8},{28,12},{1,17},{... | collective-permute-start | bytes 2064392 | tf_op jit(solution)/shard_map/ppermute | solution.py:31
  375.7 46.9 %collective-permute-start.34 = (bf16[3,64,512]{2,1,0:T(8,128)(2,1)S(1)}, bf16[3,64,512]{2,1,0:T(8,128)(2,1)S(1)}, u32[]{:S(2)}, u32[]{:S(2)}) collective-permute-start(bf16[3,64,512]{2,1,0:T(8,128)(2,1)S(1)} %get-tuple-element.165), channel_id=1, source_target_pairs={{0,24},{4,28},{8,0},{12,4},{16,8},{20,12},{24,16},{28,20},{1,25},{... | collective-permute-start | bytes 589832 | tf_op jit(solution)/shard_map/ppermute | solution.py:26
  376.3 48.0 %collective-permute-start.37 = (bf16[3,64,512]{2,1,0:T(8,128)(2,1)S(1)}, bf16[3,64,512]{2,1,0:T(8,128)(2,1)S(1)}, u32[]{:S(2)}, u32[]{:S(2)}) collective-permute-start(bf16[3,64,512]{2,1,0:T(8,128)(2,1)S(1)} %get-tuple-element.166), channel_id=1, source_target_pairs={{0,16},{4,20},{8,24},{12,28},{16,0},{20,4},{24,8},{28,12},{1,17},{... | collective-permute-start | bytes 589832 | tf_op jit(solution)/shard_map/ppermute | solution.py:26
  430.2 37.0 %collective-permute-start.49 = (bf16[448,768]{1,0:T(8,128)(2,1)S(1)}, bf16[448,768]{1,0:T(8,128)(2,1)S(1)}, u32[]{:S(2)}, u32[]{:S(2)}) collective-permute-start(bf16[448,768]{1,0:T(8,128)(2,1)S(1)} %add_convert_fusion.5), channel_id=1, source_target_pairs={{0,8},{4,12},{8,0},{12,4},{16,24},{20,28},{24,16},{28,20},{1,9},{5... | collective-permute-start | bytes 2064392 | tf_op jit(solution)/shard_map/ppermute | solution.py:31
  441.2 32.8 %collective-permute-start.44 = (bf16[208,576]{1,0:T(8,128)(2,1)S(1)}, bf16[208,576]{1,0:T(8,128)(2,1)S(1)}, u32[]{:S(2)}, u32[]{:S(2)}) collective-permute-start(bf16[208,576]{1,0:T(8,128)(2,1)S(1)} %add_convert_fusion.12), channel_id=1, source_target_pairs={{0,24},{4,28},{8,0},{12,4},{16,8},{20,12},{24,16},{28,20},{1,25},{... | collective-permute-start | bytes 718856 | tf_op jit(solution)/shard_map/ppermute | solution.py:26
  445.9 28.3 %collective-permute-start.45 = (bf16[208,576]{1,0:T(8,128)(2,1)S(1)}, bf16[208,576]{1,0:T(8,128)(2,1)S(1)}, u32[]{:S(2)}, u32[]{:S(2)}) collective-permute-start(bf16[208,576]{1,0:T(8,128)(2,1)S(1)} %add_convert_fusion.12), channel_id=1, source_target_pairs={{0,16},{4,20},{8,24},{12,28},{16,0},{20,4},{24,8},{28,12},{1,17},{... | collective-permute-start | bytes 718856 | tf_op jit(solution)/shard_map/ppermute | solution.py:26
  468.8 32.1 %collective-permute-start.50 = (bf16[896,768]{1,0:T(8,128)(2,1)}, bf16[896,768]{1,0:T(8,128)(2,1)}, u32[]{:S(2)}, u32[]{:S(2)}) collective-permute-start(bf16[896,768]{1,0:T(8,128)(2,1)} %maximum_select_fusion.10), channel_id=1, source_target_pairs={{0,4},{4,0},{8,12},{12,8},{16,20},{20,16},{24,28},{28,24},{1,5},{5... | collective-permute-start | bytes 4128776 | tf_op jit(solution)/shard_map/ppermute | solution.py:31
  (90 other events, 774.3 us)
where the time goes:
time: 515 us; the launch traced here: 510 us
  waiting for transfers between devices  152 us (30%)
  Pallas kernels  129 us (25%)
  starting transfers between devices  96.5 us (19%)
  local copies, waits for them, and re-layouts  64.3 us (12%)
  other arithmetic  54 us (10%)
  matrix products  11.1 us (2%)
    ppermute x22, waiting for transfers between devices, swap(): return lax.ppermute(array, axis, [(i, i ^ 1 << bit) for i in range(size)])  105 us
    ppermute x29, starting transfers between devices, ctx_shift(): return lax.ppermute(array, 'ctx', pairs)  79 us
    ppermute x29, waiting for transfers between devices, ctx_shift(): return lax.ppermute(array, 'ctx', pairs)  46.7 us
    pallas_call x3, Pallas kernels, attend_back(): pl.pallas_call(partial(attend_back_kernel, groups, parts, docs, rows), gr...  44.4 us
    pallas_call x1, Pallas kernels, feed_forward(): pl.pallas_call(feed_kernel, grid=(rows // tile,), in_specs=[by_rows(model...  34.6 us
    pallas_call x1, Pallas kernels, attend(): pl.pallas_call(partial(attend_kernel, groups, parts, docs, rows), grid_sp...  30.5 us
    select_n x17, other arithmetic, join(): jnp.where(mine == 0, jnp.concatenate([own, other], axis=dim), jnp.concate...  28.2 us
    ppermute x22, starting transfers between devices, swap(): return lax.ppermute(array, axis, [(i, i ^ 1 << bit) for i in range(size)])  17.5 us
  transfers between devices with their start and end apart: 51, of which 16 were waited for; matrix products, arithmetic and copies ran while one was open for 20% of the time, Pallas kernels for 16%

commit v1 on v0

--- a/solution.py
+++ b/solution.py
@@ -398,8 +398,8 @@
     slope_ref,
 ):
     f32, bf16 = jnp.float32, jnp.bfloat16
-    out_shift, gain_one, shift_one = vec_ref[0:1], vec_ref[1:2], vec_ref[2:3]
-    back_shift, gain_two, shift_two = vec_ref[3:4], vec_ref[4:5], vec_ref[5:6]
+    out_shift, gain_one, shift_one = vec_ref[2:3], vec_ref[3:4], vec_ref[4:5]
+    back_shift, gain_two, shift_two = vec_ref[5:6], vec_ref[6:7], vec_ref[7:8]
 
     @pl.when(pl.program_id(0) == 0)
     def _():
@@ -643,9 +643,8 @@
     first = gather_rest(first, first_top)
     own_weight = first[:, :shard].reshape(model, width)
     flat = first[:, shard:].reshape(fsdp, extra * width)[:, :count].astype(f32)
-    vector = lambda i: flat[:, i * shard : (i + 1) * shard].reshape(model)
-    query_shift, value_shift = vector(0), vector(1)
-    vectors = jnp.pad(jnp.stack([vector(i) for i in range(2, 8)]), ((0, 2), (0, 0)))
+    vectors = flat[:, : 8 * shard].reshape(fsdp, 8, shard).transpose(1, 0, 2).reshape(8, model)
+    query_shift, value_shift = vectors[0], vectors[1]
     in_shift = flat[:, 8 * shard :].reshape(1, -1)
 
     zero = jnp.zeros((span,), f32)
@@ -667,7 +666,7 @@
         for low in own:
             others.append(ctx_shift(low[1:], groups, parts, 0, e))
     if parts > 1:
-        in_top, others[0], others[1] = together(in_top, others[0], others[1])
+        in_top, others[0] = together(in_top, others[0])
 
     bounds = jnp.concatenate([starts, jnp.full((1,), ctx * rows, jnp.int32)])
     base = ((g - jnp.arange(groups, dtype=jnp.int32) + groups) % groups) * parts + s
@@ -684,7 +683,6 @@
     in_full = gather_rest(in_weight, in_top).reshape(model, -1)
     meta, out_full, in_full = together(meta, out_full, in_full)
     low, wide, log_total = attend(meta, own, others, groups, parts, docs, rows, heads)
-    low, qkv_held = together(low, qkv_weight)
     attended_t = jnp.zeros((groups * span, rows), bf16)
     turned = []
     for j in range(groups):
@@ -748,19 +746,20 @@
         steps.append(lambda state, bit=bit: (halve(state[0], "ctx", bit, 0),))
     state = (lower, upper)
 
-    pieces, received = [], [[] for unused in range(groups)]
+    pieces = []
     held, theirs = None, None
-
-    def send(piece):
-        pieces.append(piece)
-        for j in range(groups):
-            part = piece[:, :, j * rows : (j + 1) * rows]
-            received[j].append(ctx_shift(part, groups, parts, -j, 0) if j else part)
 
     def settle(dq, dkv, theirs):
         for other in theirs:
             dkv = dkv + other.astype(f32)
-        send(jnp.concatenate([dq[None], dkv.astype(bf16)], axis=0))
+        pieces.append(jnp.concatenate([dq[None], dkv.astype(bf16)], axis=0))
+
+    def send(piece):
+        parts_of = []
+        for j in range(groups):
+            part = piece[..., j * rows : (j + 1) * rows]
+            parts_of.append(ctx_shift(part, groups, parts, -j, 0) if j else part)
+        return parts_of
 
     for head in range(heads):
         if head and steps:
@@ -772,24 +771,27 @@
         if head:
             dq, *theirs = together(dq, *theirs)
             settle(*held, theirs)
+        if head == 1:
+            early = send(pieces[0])
+            dq, qkv_held = together(dq, qkv_weight)
+            qkv_top = gather_top(qkv_held)
+        elif head == 2:
+            if steps:
+                state = steps.pop(0)(state)
+            count = len(early)
+            dq, qkv_top, *landed = together(dq, qkv_top, *early, *state)
+            early, state = landed[:count], landed[count:]
         held = (dq, dkv)
         theirs = [ctx_shift(rest[0][e - 1], groups, parts, 0, -e) for e in range(1, parts)]
     settle(*held, theirs)
-    qkv_top = gather_top(qkv_held)
-    qkv_full = gather_rest(qkv_held, qkv_top).reshape(model, 3 * model)
     for advance in steps:
         state = advance(state)
     merged = exchange(state[0], "ctx", ctx_bits[-1])
+    late, merged = together(jnp.stack(pieces[1:], axis=1), merged)
+    late = send(late)
     for bit in reversed(ctx_bits[1:-1]):
         merged = double(merged, "ctx", bit, 0)
     other = swap(merged, "ctx", 0)
-    lower_rows = (inner_shard + shard + line_rows) // 2
-    lower = join(bit_at("ctx", 0), merged[:lower_rows], other[:lower_rows], 0)
-    wide_half = lambda m: jnp.concatenate(
-        [m[lower_rows + c * shard : lower_rows + (c + 1) * shard] for c in range(chunks)], axis=1
-    )
-    upper = join(bit_at("ctx", 0), wide_half(merged), wide_half(other), 1)
-
     d_qkv_t = jnp.stack(pieces, axis=1).reshape(width, groups * rows)
     qkv_send, qkv_sum = qkv_grads(which, slots, d_qkv_t, fsdp)
     qkv_sum = add_low(qkv_sum, swap(qkv_send, "fsdp", 0))
@@ -800,12 +802,12 @@
     for e in range(1, parts):
         wide_sum = wide_sum + ctx_shift(qkv_sum, groups, parts, 0, e).astype(f32)
     qkv_low = wide_sum.astype(bf16)
-    flat = [part for parts_of in received for part in parts_of]
-    qkv_low, *flat = together(qkv_low, *flat)
-    received = [flat[j * heads : (j + 1) * heads] for j in range(groups)]
+    qkv_full = gather_rest(qkv_held, qkv_top).reshape(model, 3 * model)
     by_group = jnp.zeros((groups,) + qkv_low.shape, bf16)
-    for j in range(groups):
-        piece = ctx_shift(qkv_low, groups, parts, -j, 0) if j else qkv_low
+    turns = [ctx_shift(qkv_low, groups, parts, -j, 0) if j else qkv_low for j in range(groups)]
+    other, *landed = together(other, *turns, *late)
+    turns, late = landed[:groups], landed[groups:]
+    for j, piece in enumerate(turns):
         by_group = lax.dynamic_update_slice(by_group, piece[None], ((g + j) % groups, 0, 0))
     natural = by_group.reshape(groups, shard + PAD, 3, span).transpose(1, 2, 0, 3)
     natural = natural.reshape(shard + PAD, 3 * model).astype(f32)
@@ -816,7 +818,7 @@
 
     natural = jnp.zeros((3, groups, heads, HD, rows), bf16)
     for j in range(groups):
-        part = jnp.stack(received[j], axis=1)[:, None]
+        part = jnp.concatenate([early[j][:, None], late[j]], axis=1)[:, None]
         natural = lax.dynamic_update_slice(natural, part, (0, (g + j) % groups, 0, 0, 0))
     input_grad = d_resid1 + lax.dot_general(
         natural.reshape(3 * model, rows),
@@ -824,6 +826,13 @@
         (((0,), (1,)), ((), ())),
         preferred_element_type=f32,
     )
+
+    lower_rows = (inner_shard + shard + line_rows) // 2
+    lower = join(bit_at("ctx", 0), merged[:lower_rows], other[:lower_rows], 0)
+    wide_half = lambda m: jnp.concatenate(
+        [m[lower_rows + c * shard : lower_rows + (c + 1) * shard] for c in range(chunks)], axis=1
+    )
+    upper = join(bit_at("ctx", 0), wide_half(merged), wide_half(other), 1)
 
     ends = inner_shard + shard
     flat = lower[ends:].reshape(-1).astype(f32)

time: 515 us -> 490 us (0.951)
  the two profiles are of different devices: /device:TPU:28 before, /device:TPU:0 now
where the time goes in v1:
time: 490 us; the launch traced here: 483 us
  waiting for transfers between devices  168 us (34%)
  Pallas kernels  137 us (28%)
  local copies, waits for them, and re-layouts  55.6 us (11%)
  other arithmetic  55 us (11%)
  starting transfers between devices  53.1 us (11%)
  matrix products  11.1 us (2%)
    ppermute x26, waiting for transfers between devices, ctx_shift(): return lax.ppermute(array, 'ctx', pairs)  87.9 us
    ppermute x22, waiting for transfers between devices, swap(): return lax.ppermute(array, axis, [(i, i ^ 1 << bit) for i in range(size)])  80.6 us
    pallas_call x3, Pallas kernels, attend_back(): pl.pallas_call(partial(attend_back_kernel, groups, parts, docs, rows), gr...  48.7 us
    ppermute x26, starting transfers between devices, ctx_shift(): return lax.ppermute(array, 'ctx', pairs)  36 us
    pallas_call x1, Pallas kernels, feed_forward(): pl.pallas_call(feed_kernel, grid=(rows // tile,), in_specs=[by_rows(model...  34.6 us
    pallas_call x1, Pallas kernels, attend(): pl.pallas_call(partial(attend_kernel, groups, parts, docs, rows), grid_sp...  34.4 us
    select_n x17, other arithmetic, join(): jnp.where(mine == 0, jnp.concatenate([own, other], axis=dim), jnp.concate...  26.7 us
    ppermute x22, starting transfers between devices, swap(): return lax.ppermute(array, axis, [(i, i ^ 1 << bit) for i in range(size)])  17.1 us
  transfers between devices with their start and end apart: 48, of which 18 were waited for; matrix products, arithmetic and copies ran while one was open for 18% of the time, Pallas kernels for 19%

profile of v1, /device:TPU:0, one launch (start us, length us, event | category | flops | bytes accessed | tf_op | source)
XLA Modules:
  0.0 483.0 jit_solution(6573586859801782505)
XLA Ops:
  14.8 6.0 %collective-permute-done = bf16[208,576]{0,1:T(8,128)(2,1)S(1)} collective-permute-done((bf16[208,576]{0,1:T(8,128)(2,1)S(1)}, bf16[208,576]{0,1:T(8,128)(2,1)S(1)}, u32[]{:S(2)}, u32[]{:S(2)}) %collective-permute-start) | collective-permute-done | bytes 239648 | tf_op jit(solution)/shard_map/ppermute | solution.py:31
  39.6 9.2 %collective-permute-done.5.refs_4_ = bf16[2,3,64,512]{3,2,1,0:T(8,128)(2,1)S(1)} collective-permute-done((bf16[2,3,64,512]{3,2,1,0:T(8,128)(2,1)}, bf16[2,3,64,512]{3,2,1,0:T(8,128)(2,1)S(1)}, u32[]{:S(2)}, u32[]{:S(2)}) %collective-permute-start.5) | collective-permute-done | bytes 393248 | tf_op jit(solution)/shard_map/ppermute | solution.py:26
  75.5 8.7 %collective-permute-done.16 = bf16[768,768]{1,0:T(8,128)(2,1)S(1)} collective-permute-done((bf16[768,768]{1,0:T(8,128)(2,1)S(1)}, bf16[768,768]{1,0:T(8,128)(2,1)S(1)}, u32[]{:S(2)}, u32[]{:S(2)}) %collective-permute-start.16) | collective-permute-done | bytes 1179680 | tf_op jit(solution)/shard_map/ppermute | solution.py:31
  96.4 34.4 %attend.1 = (bf16[3,64,2048]{2,1,0:T(8,128)(2,1)}, f32[3,64,2048]{2,1,0:T(8,128)}, f32[3,1,2048]{2,1,0:T(1,128)}) custom-call(s32[18]{0:T(128)} %pad_add_fusion.2.meta, bf16[3,3,64,512]{3,2,1,0:T(8,128)(2,1)} %bitcast.193, bf16[3,3,64,512]{3,2,1,0:T(8,128)(2,1)} %bitcast.197, bf16[3,3,64,512]{3,2,1,0:T(8,128)(2,1)} %bitcast.201, ...), custom_call_target="tpu_custom_call" | custom-call | flops 17999998976 | bytes 60000000 | tf_op jit(solution)/shard_map/attend/pallas_call | solution.py:282
  132.1 7.1 %collective-permute-start.13 = (bf16[3,64,512]{2,1,0:T(8,128)(2,1)S(1)}, bf16[3,64,512]{2,1,0:T(8,128)(2,1)S(1)}, u32[]{:S(2)}, u32[]{:S(2)}) collective-permute-start(bf16[3,64,512]{2,1,0:T(8,128)(2,1)S(1)} %get-tuple-element.181), channel_id=1, source_target_pairs={{0,24},{4,28},{8,0},{12,4},{16,8},{20,12},{24,16},{28,20},{1,25},{... | collective-permute-start | bytes 589832 | tf_op jit(solution)/shard_map/ppermute | solution.py:26
  145.4 7.6 %collective-permute-done.14 = bf16[3,64,512]{2,1,0:T(8,128)(2,1)S(1)} collective-permute-done((bf16[3,64,512]{2,1,0:T(8,128)(2,1)S(1)}, bf16[3,64,512]{2,1,0:T(8,128)(2,1)S(1)}, u32[]{:S(2)}, u32[]{:S(2)}) %collective-permute-start.14) | collective-permute-done | bytes 196640 | tf_op jit(solution)/shard_map/ppermute | solution.py:26
  154.1 34.6 %feed_forward.1 = (bf16[512,768]{1,0:T(8,128)(2,1)}, f32[512,768]{1,0:T(8,128)}, bf16[768,512]{1,0:T(8,128)(2,1)}, bf16[4,512,192]{2,1,0:T(8,128)(2,1)}, bf16[4,...) custom-call(bf16[512,768]{1,0:T(8,128)(2,1)} %bitcast.237, ...), custom_call_target="tpu_custom_call" | custom-call | flops 10871635968 | bytes 30000000 | tf_op jit(solution)/shard_map/feed_forward/pallas_call | solution.py:477
  192.7 12.1 %weight_grads.1 = (bf16[2,1024,768]{2,1,0:T(8,128)(2,1)}, bf16[2,192,3072]{2,1,0:T(8,128)(2,1)}, bf16[2,1024,768]{2,1,0:T(8,128)(2,1)}, bf16[2,192,3072]{2,1,0:T(8,128)(2,1)}) custom-call(s32[2]{0:T(128)} %pad_add_fusion.3.which, bf16[4,512,768]{2,1,0:T(8,128)(2,1)} %get-tuple-element.104.refs_0_.refs_4_, ...), custom_call_target="tpu_custom_call" | custom-call | flops 5435817984 | bytes 25000000 | tf_op jit(solution)/shard_map/weight_grads/pallas_call | solution.py:534
  222.7 4.9 %collective-permute-start.20 = (bf16[1,1024,768]{2,1,0:T(8,128)(2,1)}, bf16[1,1024,768]{2,1,0:T(8,128)(2,1)}, u32[]{:S(2)}, u32[]{:S(2)}) collective-permute-start(bf16[1,1024,768]{2,1,0:T(8,128)(2,1)} %constant_dynamic-slice_fusion.11), channel_id=1, source_target_pairs={{0,2},{1,3},{2,0},{3,1},{4,6},{5,7},{6,4},{7,5},{8,10},{9,11},{10,... | collective-permute-start | bytes 4718600 | tf_op jit(solution)/shard_map/ppermute | solution.py:31
  228.5 16.2 %attend_back.5 = (bf16[64,2048]{1,0:T(8,128)(2,1)}, f32[2,64,2048]{2,1,0:T(8,128)}, bf16[1,2,64,2048]{3,2,1,0:T(8,128)(2,1)}) custom-call(s32[18]{0:T(128)} %pad_add_fusion.2.meta, bf16[3,3,64,512]{3,2,1,0:T(8,128)(2,1)} %bitcast.194, bf16[3,3,64,512]{3,2,1,0:T(8,128)(2,1)} %bitcast.198, bf16[3,3,64,512]{3,2,1,0:T(8,128)(2,1)} %bitcast.202, ...), custom_call_target="tpu_custom_call" | custom-call | flops 15000000512 | bytes 20000000 | tf_op jit(solution)/shard_map/attend_back/pallas_call | solution.py:329
  244.7 5.9 %collective-permute-done.21 = bf16[2,192,1536]{2,1,0:T(8,128)(2,1)} collective-permute-done((bf16[2,192,1536]{2,1,0:T(8,128)(2,1)}, bf16[2,192,1536]{2,1,0:T(8,128)(2,1)}, u32[]{:S(2)}, u32[]{:S(2)}) %collective-permute-start.21) | collective-permute-done | bytes 1179680 | tf_op jit(solution)/shard_map/ppermute | solution.py:31
  253.5 7.9 %collective-permute-done.20 = bf16[1,1024,768]{2,1,0:T(8,128)(2,1)} collective-permute-done((bf16[1,1024,768]{2,1,0:T(8,128)(2,1)}, bf16[1,1024,768]{2,1,0:T(8,128)(2,1)}, u32[]{:S(2)}, u32[]{:S(2)}) %collective-permute-start.20) | collective-permute-done | bytes 1572896 | tf_op jit(solution)/shard_map/ppermute | solution.py:31
  264.4 16.3 %attend_back.4 = (bf16[64,2048]{1,0:T(8,128)(2,1)}, f32[2,64,2048]{2,1,0:T(8,128)}, bf16[1,2,64,2048]{3,2,1,0:T(8,128)(2,1)}) custom-call(s32[18]{0:T(128)} %pad_add_fusion.2.meta, bf16[3,3,64,512]{3,2,1,0:T(8,128)(2,1)} %bitcast.195, bf16[3,3,64,512]{3,2,1,0:T(8,128)(2,1)} %bitcast.199, bf16[3,3,64,512]{3,2,1,0:T(8,128)(2,1)} %bitcast.203, ...), custom_call_target="tpu_custom_call" | custom-call | flops 15000000512 | bytes 20000000 | tf_op jit(solution)/shard_map/attend_back/pallas_call | solution.py:329
  288.2 7.5 %collective-permute-done.23 = bf16[1,192,1536]{2,1,0:T(8,128)(2,1)S(1)} collective-permute-done((bf16[1,192,1536]{2,1,0:T(8,128)(2,1)S(1)}, bf16[1,192,1536]{2,1,0:T(8,128)(2,1)S(1)}, u32[]{:S(2)}, u32[]{:S(2)}) %collective-permute-start.23) | collective-permute-done | bytes 589856 | tf_op jit(solution)/shard_map/ppermute | solution.py:31
  296.9 4.5 collective-permute-done.22
  301.6 16.2 %attend_back.3 = (bf16[64,2048]{1,0:T(8,128)(2,1)}, f32[2,64,2048]{2,1,0:T(8,128)}, bf16[1,2,64,2048]{3,2,1,0:T(8,128)(2,1)}) custom-call(s32[18]{0:T(128)} %pad_add_fusion.2.meta, bf16[3,3,64,512]{3,2,1,0:T(8,128)(2,1)} %bitcast.196, bf16[3,3,64,512]{3,2,1,0:T(8,128)(2,1)} %bitcast.200, bf16[3,3,64,512]{3,2,1,0:T(8,128)(2,1)} %bitcast.204, ...), custom_call_target="tpu_custom_call" | custom-call | flops 15000000512 | bytes 20000000 | tf_op jit(solution)/shard_map/attend_back/pallas_call | solution.py:329
  320.4 8.3 %collective-permute-done.34 = bf16[2,64,2048]{2,1,0:T(8,128)(2,1)S(1)} collective-permute-done((bf16[2,64,2048]{2,1,0:T(8,128)(2,1)}, bf16[2,64,2048]{2,1,0:T(8,128)(2,1)S(1)}, u32[]{:S(2)}, u32[]{:S(2)}) %collective-permute-start.34) | collective-permute-done | bytes 524320 | tf_op jit(solution)/shard_map/ppermute | solution.py:26
  331.7 4.6 collective-permute-done.32
  339.9 7.6 %qkv_grads.1 = (bf16[2,208,576]{2,1,0:T(8,128)(2,1)}, bf16[2,208,576]{2,1,0:T(8,128)(2,1)}) custom-call(s32[2]{0:T(128)} %pad_add_fusion.3.which, bf16[512,768]{1,0:T(8,128)(2,1)} %bitcast.238, bf16[512,768]{1,0:T(8,128)(2,1)} %collective-permute-done.7.refs_1_, bf16[512,768]{1,0:T(8,128)(2,1)} %collective-permute-done.8.refs_2_, ...), custom_call_target="tpu_custom_call" | custom-call | flops 1811939328 | bytes 8000000 | tf_op jit(solution)/shard_map/qkv_grads/pallas_call | solution.py:573
  349.9 18.8 %collective-permute-done.35 = bf16[448,768]{1,0:T(8,128)(2,1)S(1)} collective-permute-done((bf16[448,768]{1,0:T(8,128)(2,1)}, bf16[448,768]{1,0:T(8,128)(2,1)S(1)}, u32[]{:S(2)}, u32[]{:S(2)}) %collective-permute-start.35) | collective-permute-done | bytes 688160 | tf_op jit(solution)/shard_map/ppermute | solution.py:31
  372.0 15.4 %collective-permute-done.36 = bf16[448,768]{1,0:T(8,128)(2,1)S(1)} collective-permute-done((bf16[448,768]{1,0:T(8,128)(2,1)S(1)}, bf16[448,768]{1,0:T(8,128)(2,1)S(1)}, u32[]{:S(2)}, u32[]{:S(2)}) %collective-permute-start.36) | collective-permute-done | bytes 688160 | tf_op jit(solution)/shard_map/ppermute | solution.py:31
  394.2 31.8 %collective-permute-done.40 = bf16[208,576]{1,0:T(8,128)(2,1)S(1)} collective-permute-done((bf16[208,576]{1,0:T(8,128)(2,1)S(1)}, bf16[208,576]{1,0:T(8,128)(2,1)S(1)}, u32[]{:S(2)}, u32[]{:S(2)}) %collective-permute-start.40) | collective-permute-done | bytes 239648 | tf_op jit(solution)/shard_map/ppermute | solution.py:26
  433.9 5.9 %collective-permute-done.46 = bf16[3,2,64,512]{3,2,0,1:T(8,128)(2,1)S(1)} collective-permute-done((bf16[3,2,64,512]{3,2,0,1:T(8,128)(2,1)S(1)}, bf16[3,2,64,512]{3,2,0,1:T(8,128)(2,1)S(1)}, u32[]{:S(2)}, u32[]{:S(2)}) %collective-permute-start.46) | collective-permute-done | bytes 393248 | tf_op jit(solution)/shard_map/ppermute | solution.py:26
  442.9 17.3 %collective-permute-done.42 = bf16[208,576]{1,0:T(8,128)(2,1)S(1)} collective-permute-done((bf16[208,576]{1,0:T(8,128)(2,1)S(1)}, bf16[208,576]{1,0:T(8,128)(2,1)S(1)}, u32[]{:S(2)}, u32[]{:S(2)}) %collective-permute-start.42) | collective-permute-done | bytes 239648 | tf_op jit(solution)/shard_map/ppermute | solution.py:26
  (364 shorter events, 171.7 us)
Async XLA Ops:
  0.6 63.6 %collective-permute-start.7 = (bf16[512,768]{1,0:T(8,128)(2,1)}, bf16[512,768]{1,0:T(8,128)(2,1)}, u32[]{:S(2)}, u32[]{:S(2)}) collective-permute-start(bf16[512,768]{1,0:T(8,128)(2,1)} %bitcast.234), channel_id=1, source_target_pairs={{0,8},{4,12},{8,16},{12,20},{16,24},{20,28},{24,0},{28,4},{1,9},{5... | collective-permute-start | bytes 2359304 | tf_op jit(solution)/shard_map/ppermute | solution.py:26
  3.8 62.8 %collective-permute-start.8 = (bf16[512,768]{1,0:T(8,128)(2,1)}, bf16[512,768]{1,0:T(8,128)(2,1)}, u32[]{:S(2)}, u32[]{:S(2)}) collective-permute-start(bf16[512,768]{1,0:T(8,128)(2,1)} %bitcast.235), channel_id=1, source_target_pairs={{0,16},{4,20},{8,24},{12,28},{16,0},{20,4},{24,8},{28,12},{1,17},{... | collective-permute-start | bytes 2359304 | tf_op jit(solution)/shard_map/ppermute | solution.py:26
  6.3 63.7 %collective-permute-start.9 = (bf16[512,768]{1,0:T(8,128)(2,1)}, bf16[512,768]{1,0:T(8,128)(2,1)}, u32[]{:S(2)}, u32[]{:S(2)}) collective-permute-start(bf16[512,768]{1,0:T(8,128)(2,1)} %bitcast.236), channel_id=1, source_target_pairs={{0,24},{4,28},{8,0},{12,4},{16,8},{20,12},{24,16},{28,20},{1,25},{... | collective-permute-start | bytes 2359304 | tf_op jit(solution)/shard_map/ppermute | solution.py:26
  22.3 28.4 %collective-permute-start.3 = (bf16[192,3072]{1,0:T(8,128)(2,1)S(1)}, bf16[192,3072]{1,0:T(8,128)(2,1)S(1)}, u32[]{:S(2)}, u32[]{:S(2)}) collective-permute-start(bf16[192,3072]{1,0:T(8,128)(2,1)S(1)} %copy-done.4), channel_id=1, source_target_pairs={{0,2},{1,3},{2,0},{3,1},{4,6},{5,7},{6,4},{7,5},{8,10},{9,11},{10,... | collective-permute-start | bytes 3538952 | tf_op jit(solution)/shard_map/ppermute | solution.py:31
  52.6 36.2 %collective-permute-start.6 = (bf16[2,192,3072]{2,1,0:T(8,128)(2,1)}, bf16[2,192,3072]{2,1,0:T(8,128)(2,1)}, u32[]{:S(2)}, u32[]{:S(2)}) collective-permute-start(bf16[2,192,3072]{2,1,0:T(8,128)(2,1)} %maximum_select_fusion.4), channel_id=1, source_target_pairs={{0,1},{1,0},{2,3},{3,2},{4,5},{5,4},{6,7},{7,6},{8,9},{9,8},{10,11... | collective-permute-start | bytes 7077896 | tf_op jit(solution)/shard_map/ppermute | solution.py:31
  57.5 26.7 %collective-permute-start.16 = (bf16[768,768]{1,0:T(8,128)(2,1)S(1)}, bf16[768,768]{1,0:T(8,128)(2,1)S(1)}, u32[]{:S(2)}, u32[]{:S(2)}) collective-permute-start(bf16[768,768]{1,0:T(8,128)(2,1)S(1)} %copy-done.3), channel_id=1, source_target_pairs={{0,2},{1,3},{2,0},{3,1},{4,6},{5,7},{6,4},{7,5},{8,10},{9,11},{10,... | collective-permute-start | bytes 3538952 | tf_op jit(solution)/shard_map/ppermute | solution.py:31
  66.6 28.4 %collective-permute-start.10 = (bf16[2,3,64,512]{3,2,1,0:T(8,128)(2,1)S(1)}, bf16[2,3,64,512]{3,2,1,0:T(8,128)(2,1)S(1)}, u32[]{:S(2)}, u32[]{:S(2)}) collective-permute-start(bf16[2,3,64,512]{3,2,1,0:T(8,128)(2,1)S(1)} %bitcast.187), channel_id=1, source_target_pairs={{0,4},{4,0},{8,12},{12,8},{16,20},{20,16},{24,28},{28,24},{1,5},{5... | collective-permute-start | bytes 1179656 | tf_op jit(solution)/shard_map/ppermute | solution.py:26
  70.1 24.8 %collective-permute-start.11 = (bf16[2,3,64,512]{3,2,1,0:T(8,128)(2,1)S(1)}, bf16[2,3,64,512]{3,2,1,0:T(8,128)(2,1)S(1)}, u32[]{:S(2)}, u32[]{:S(2)}) collective-permute-start(bf16[2,3,64,512]{3,2,1,0:T(8,128)(2,1)S(1)} %bitcast.188), channel_id=1, source_target_pairs={{0,4},{4,0},{8,12},{12,8},{16,20},{20,16},{24,28},{28,24},{1,5},{5... | collective-permute-start | bytes 1179656 | tf_op jit(solution)/shard_map/ppermute | solution.py:26
  86.0 53.8 %collective-permute-start.17 = (bf16[2,768,768]{2,1,0:T(8,128)(2,1)}, bf16[2,768,768]{2,1,0:T(8,128)(2,1)}, u32[]{:S(2)}, u32[]{:S(2)}) collective-permute-start(bf16[2,768,768]{2,1,0:T(8,128)(2,1)} %maximum_select_fusion.6), channel_id=1, source_target_pairs={{0,1},{1,0},{2,3},{3,2},{4,5},{5,4},{6,7},{7,6},{8,9},{9,8},{10,11... | collective-permute-start | bytes 7077896 | tf_op jit(solution)/shard_map/ppermute | solution.py:31
  221.5 29.2 %collective-permute-start.21 = (bf16[2,192,1536]{2,1,0:T(8,128)(2,1)}, bf16[2,192,1536]{2,1,0:T(8,128)(2,1)}, u32[]{:S(2)}, u32[]{:S(2)}) collective-permute-start(bf16[2,192,1536]{2,1,0:T(8,128)(2,1)} %constant_dynamic-slice_fusion.10), channel_id=1, source_target_pairs={{0,4},{4,0},{8,12},{12,8},{16,20},{20,16},{24,28},{28,24},{1,5},{5... | collective-permute-start | bytes 3538952 | tf_op jit(solution)/shard_map/ppermute | solution.py:31
  222.7 38.8 %collective-permute-start.20 = (bf16[1,1024,768]{2,1,0:T(8,128)(2,1)}, bf16[1,1024,768]{2,1,0:T(8,128)(2,1)}, u32[]{:S(2)}, u32[]{:S(2)}) collective-permute-start(bf16[1,1024,768]{2,1,0:T(8,128)(2,1)} %constant_dynamic-slice_fusion.11), channel_id=1, source_target_pairs={{0,2},{1,3},{2,0},{3,1},{4,6},{5,7},{6,4},{7,5},{8,10},{9,11},{10,... | collective-permute-start | bytes 4718600 | tf_op jit(solution)/shard_map/ppermute | solution.py:31
  244.7 36.1 %collective-permute-start.28 = (bf16[2,64,2048]{2,1,0:T(8,128)(2,1)}, bf16[2,64,2048]{2,1,0:T(8,128)(2,1)}, u32[]{:S(2)}, u32[]{:S(2)}) collective-permute-start(bf16[2,64,2048]{2,1,0:T(8,128)(2,1)} %bitcast.240), channel_id=1, source_target_pairs={{0,4},{4,0},{8,12},{12,8},{16,20},{20,16},{24,28},{28,24},{1,5},{5... | collective-permute-start | bytes 1572872 | tf_op jit(solution)/shard_map/ppermute | solution.py:26
  286.2 31.6 %collective-permute-start.27 = (bf16[2,64,2048]{2,1,0:T(8,128)(2,1)}, bf16[2,64,2048]{2,1,0:T(8,128)(2,1)}, u32[]{:S(2)}, u32[]{:S(2)}) collective-permute-start(bf16[2,64,2048]{2,1,0:T(8,128)(2,1)} %bitcast.57), channel_id=1, source_target_pairs={{0,4},{4,0},{8,12},{12,8},{16,20},{20,16},{24,28},{28,24},{1,5},{5... | collective-permute-start | bytes 1572872 | tf_op jit(solution)/shard_map/ppermute | solution.py:26
  287.1 44.6 %collective-permute-start.30 = (bf16[3,64,512]{2,1,0:T(8,128)(2,1)}, bf16[3,64,512]{2,1,0:T(8,128)(2,1)S(1)}, u32[]{:S(2)}, u32[]{:S(2)}) collective-permute-start(bf16[3,64,512]{2,1,0:T(8,128)(2,1)} %get-tuple-element.173), channel_id=1, source_target_pairs={{0,24},{4,28},{8,0},{12,4},{16,8},{20,12},{24,16},{28,20},{1,25},{... | collective-permute-start | bytes 589832 | tf_op jit(solution)/shard_map/ppermute | solution.py:26
  287.4 44.3 %collective-permute-start.31 = (bf16[3,64,512]{2,1,0:T(8,128)(2,1)}, bf16[3,64,512]{2,1,0:T(8,128)(2,1)S(1)}, u32[]{:S(2)}, u32[]{:S(2)}) collective-permute-start(bf16[3,64,512]{2,1,0:T(8,128)(2,1)} %get-tuple-element.174), channel_id=1, source_target_pairs={{0,16},{4,20},{8,24},{12,28},{16,0},{20,4},{24,8},{28,12},{1,17},{... | collective-permute-start | bytes 589832 | tf_op jit(solution)/shard_map/ppermute | solution.py:26
  295.7 40.7 %collective-permute-start.29 = (bf16[192,2304]{1,0:T(8,128)(2,1)S(1)}, bf16[192,2304]{1,0:T(8,128)(2,1)}, u32[]{:S(2)}, u32[]{:S(2)}) collective-permute-start(bf16[192,2304]{1,0:T(8,128)(2,1)S(1)} %copy-done.1), channel_id=1, source_target_pairs={{0,2},{1,3},{2,0},{3,1},{4,6},{5,7},{6,4},{7,5},{8,10},{9,11},{10,... | collective-permute-start | bytes 2654216 | tf_op jit(solution)/shard_map/ppermute | solution.py:31
  339.0 29.7 %collective-permute-start.35 = (bf16[448,768]{1,0:T(8,128)(2,1)}, bf16[448,768]{1,0:T(8,128)(2,1)S(1)}, u32[]{:S(2)}, u32[]{:S(2)}) collective-permute-start(bf16[448,768]{1,0:T(8,128)(2,1)} %add_convert_fusion.6), channel_id=1, source_target_pairs={{0,16},{4,20},{8,24},{12,28},{16,0},{20,4},{24,8},{28,12},{1,17},{... | collective-permute-start | bytes 2064392 | tf_op jit(solution)/shard_map/ppermute | solution.py:31
  349.2 81.7 %collective-permute-start.47 = (bf16[2,192,2304]{2,1,0:T(8,128)(2,1)S(1)}, bf16[2,192,2304]{2,1,0:T(8,128)(2,1)S(1)}, u32[]{:S(2)}, u32[]{:S(2)}) collective-permute-start(bf16[2,192,2304]{2,1,0:T(8,128)(2,1)S(1)} %maximum_select_fusion.8), channel_id=1, source_target_pairs={{0,1},{1,0},{2,3},{3,2},{4,5},{5,4},{6,7},{7,6},{8,9},{9,8},{10,11... | collective-permute-start | bytes 5308424 | tf_op jit(solution)/shard_map/ppermute | solution.py:31
  388.0 72.2 %collective-permute-start.37 = (bf16[896,768]{1,0:T(8,128)(2,1)S(1)}, bf16[896,768]{1,0:T(8,128)(2,1)S(1)}, u32[]{:S(2)}, u32[]{:S(2)}) collective-permute-start(bf16[896,768]{1,0:T(8,128)(2,1)S(1)} %maximum_select_fusion.10), channel_id=1, source_target_pairs={{0,4},{4,0},{8,12},{12,8},{16,20},{20,16},{24,28},{28,24},{1,5},{5... | collective-permute-start | bytes 4128776 | tf_op jit(solution)/shard_map/ppermute | solution.py:31
  390.9 35.1 %collective-permute-start.40 = (bf16[208,576]{1,0:T(8,128)(2,1)S(1)}, bf16[208,576]{1,0:T(8,128)(2,1)S(1)}, u32[]{:S(2)}, u32[]{:S(2)}) collective-permute-start(bf16[208,576]{1,0:T(8,128)(2,1)S(1)} %fusion.7), channel_id=1, source_target_pairs={{0,4},{4,0},{8,12},{12,8},{16,20},{20,16},{24,28},{28,24},{1,5},{5... | collective-permute-start | bytes 718856 | tf_op jit(solution)/shard_map/ppermute | solution.py:26
  391.9 35.7 %collective-permute-start.44 = (bf16[3,2,64,512]{3,2,0,1:T(8,128)(2,1)S(1)}, bf16[3,2,64,512]{3,2,0,1:T(8,128)(2,1)S(1)}, u32[]{:S(2)}, u32[]{:S(2)}) collective-permute-start(bf16[3,2,64,512]{3,2,0,1:T(8,128)(2,1)S(1)} %get-tuple-element.165), channel_id=1, source_target_pairs={{0,24},{4,28},{8,0},{12,4},{16,8},{20,12},{24,16},{28,20},{1,25},{... | collective-permute-start | bytes 1179656 | tf_op jit(solution)/shard_map/ppermute | solution.py:26
  394.2 36.7 %collective-permute-start.45 = (bf16[3,2,64,512]{3,2,0,1:T(8,128)(2,1)S(1)}, bf16[3,2,64,512]{3,2,0,1:T(8,128)(2,1)S(1)}, u32[]{:S(2)}, u32[]{:S(2)}) collective-permute-start(bf16[3,2,64,512]{3,2,0,1:T(8,128)(2,1)S(1)} %get-tuple-element.164), channel_id=1, source_target_pairs={{0,16},{4,20},{8,24},{12,28},{16,0},{20,4},{24,8},{28,12},{1,17},{... | collective-permute-start | bytes 1179656 | tf_op jit(solution)/shard_map/ppermute | solution.py:26
  430.9 29.3 %collective-permute-start.42 = (bf16[208,576]{1,0:T(8,128)(2,1)S(1)}, bf16[208,576]{1,0:T(8,128)(2,1)S(1)}, u32[]{:S(2)}, u32[]{:S(2)}) collective-permute-start(bf16[208,576]{1,0:T(8,128)(2,1)S(1)} %add_convert_fusion.12), channel_id=1, source_target_pairs={{0,16},{4,20},{8,24},{12,28},{16,0},{20,4},{24,8},{28,12},{1,17},{... | collective-permute-start | bytes 718856 | tf_op jit(solution)/shard_map/ppermute | solution.py:26
  430.9 29.3 %collective-permute-start.43 = (bf16[208,576]{1,0:T(8,128)(2,1)S(1)}, bf16[208,576]{1,0:T(8,128)(2,1)S(1)}, u32[]{:S(2)}, u32[]{:S(2)}) collective-permute-start(bf16[208,576]{1,0:T(8,128)(2,1)S(1)} %add_convert_fusion.12), channel_id=1, source_target_pairs={{0,8},{4,12},{8,16},{12,20},{16,24},{20,28},{24,0},{28,4},{1,9},{5... | collective-permute-start | bytes 718856 | tf_op jit(solution)/shard_map/ppermute | solution.py:26
  (92 other events, 619.9 us)
